TPU v7x, 32 devices: a whole 2x2x4 slice. The times are simulated.
32 devices in a mesh: dp: 4 (over y, core), wide: 8 (over z, x).
Axes of the slice: x: 2, y: 2, z: 4, core: 2. Of those that a mesh axis runs over, the one named last changes fastest.
Arguments:
- frames: bfloat16 [4, 2, 16, 64, 512], P('dp', None, 'wide'), may hold values from -6 to 6
- conv_weight: bfloat16 [3, 512, 512], replicated, may hold values from -0.15625 to 0.15625
- embed_weight: bfloat16 [512, 1536], replicated, may hold values from -0.25 to 0.25
- query_weight: bfloat16 [1536, 1536], P('wide'), may hold values from -3 to 3
- key_weight: bfloat16 [1536, 1536], P('wide'), may hold values from -3 to 3
- value_weight: bfloat16 [1536, 1536], P('wide'), may hold values from -0.15625 to 0.15625
- output_weight: bfloat16 [1536, 1536], P('wide'), may hold values from -0.15625 to 0.15625
- out_grad: bfloat16 [4, 4, 16, 64, 1536], P('dp', None, 'wide'), may hold values from -0.119628906 to 0.119628906
- bucket_owner: int32 [16], replicated, may hold values from 0 to 3, as said below
- clip_bucket: int32 [4, 2], replicated, may hold values from 0 to 15, as said below
- clip_frames: int32 [4, 2], replicated, may hold values from 4 to 16, as said below
- clip_grid: int32 [4, 2, 2], replicated, may hold values from 2 to 32, as said below
Outputs:
- block_out: bfloat16 [4, 4, 16, 64, 1536], P('dp', None, 'wide')
- grad_query: float32 [1536, 1536], P('wide')
- grad_key: float32 [1536, 1536], P('wide')
- grad_value: float32 [1536, 1536], P('wide')
- grad_output: float32 [1536, 1536], P('wide')
Inputs may be any that keep to these rules, and one draw needn't show every extreme that they name: `bucket_owner`: each owner has exactly 4 buckets. `clip_bucket`: the 2 clips of one group have buckets of different owners; some owner has a clip of every group. `clip_frames`: some clip has all 16 frames. `clip_grid`: the product of a clip's two entries is at most 64, and equals it for some clip.
All inputs are finite; a program needn't handle non-finite values.
Results may differ from a plain program's by a relative error of at most 0.025.
Values may be sent and summed in bfloat16 or wider, within the bound.
A program may use at most 128 MiB of HBM per device.

v0:
```python
import math

import jax
import jax.numpy as jnp
from jax import lax
from jax.sharding import PartitionSpec as P

HEAD_DIM = 128


EPS = 1e-06
masked_score = -1e30


def from_behind(shard, axis, by):
    count = lax.axis_size(axis)
    pairs = [(i, i + by) for i in range(count) if 0 <= i + by < count]
    return lax.ppermute(shard, axis, pairs)


def as_sent(shard):
    return jax.tree.map(lambda a: a.astype(jnp.bfloat16) if a.dtype == jnp.float32 else a, shard)


def layer_norm(values):
    floats = values.astype(jnp.float32)
    center = floats - jnp.mean(floats, axis=-1, keepdims=True)
    spread = jnp.mean(center * center, axis=-1, keepdims=True)
    return (center * lax.rsqrt(spread + EPS)).astype(jnp.bfloat16)


def body(
    frames,
    conv_weight,
    embed_weight,
    query_weight,
    key_weight,
    value_weight,
    output_weight,
    out_grad,
    bucket_owner,
    clip_bucket,
    clip_frames,
    clip_grid,
):
    scale = 1.0 / math.sqrt(HEAD_DIM)
    groups = lax.axis_size("dp")
    my_group = lax.axis_index("dp")
    my_slab = lax.axis_index("wide")
    frame_slab = frames[0]
    clip_count, slab_frames, site_count, channels = frame_slab.shape
    model_width = embed_weight.shape[1]
    head_count = model_width // HEAD_DIM
    earlier = from_behind(frame_slab, "wide", 1)
    joined = jnp.concatenate([earlier, frame_slab], axis=1)
    active = jax.nn.silu(joined.astype(jnp.float32)).astype(jnp.bfloat16)
    summed = frame_slab.astype(jnp.float32)
    for offset in range(3):
        moved = active[:, slab_frames - offset : 2 * slab_frames - offset].reshape(-1, channels)
        summed = summed + jnp.dot(
            moved, conv_weight[offset], preferred_element_type=jnp.float32
        ).reshape(summed.shape)
    encoded = summed.astype(jnp.bfloat16)
    bucket_table = (
        clip_bucket[:, :, None] == jnp.arange(bucket_owner.shape[0], dtype=jnp.int32)
    ).astype(jnp.int32)
    owners = jnp.sum(bucket_table * bucket_owner, axis=-1)
    group_index = jnp.arange(groups, dtype=jnp.int32)
    mine = (group_index == my_group).astype(jnp.int32)
    my_owners = jnp.sum(mine[:, None] * owners, axis=0)
    send_table = (my_owners[None, :] == group_index[:, None]).astype(jnp.bfloat16)
    recv_table = (owners == my_group).astype(jnp.int32)
    grid_tokens = clip_grid[..., 0] * clip_grid[..., 1]
    live_frames = jnp.sum(recv_table * clip_frames, axis=1)
    live_tokens = jnp.sum(recv_table * grid_tokens, axis=1)
    key_tokens = jnp.where(live_tokens > 0, live_tokens, site_count)
    frame_pos = my_slab * slab_frames + jnp.arange(slab_frames, dtype=jnp.int32)
    site_pos = jnp.arange(site_count, dtype=jnp.int32)
    live = (frame_pos[None, :, None] < live_frames[:, None, None]) & (
        site_pos[None, None, :] < live_tokens[:, None, None]
    )
    live_rows = live.reshape(-1)
    embedded = jnp.dot(
        encoded.reshape(-1, channels), embed_weight, preferred_element_type=jnp.float32
    ).astype(jnp.bfloat16)
    embedded = embedded.reshape(clip_count, slab_frames, site_count, model_width)
    tokens = lax.all_to_all(
        jnp.einsum(
            "oc,cfsw->ofsw", send_table, embedded, preferred_element_type=jnp.float32
        ).astype(jnp.bfloat16),
        "dp",
        split_axis=0,
        concat_axis=0,
        tiled=True,
    ).reshape(-1, model_width)
    normed = layer_norm(tokens)
    weight_rows = (
        lax.all_gather(query_weight, "wide", axis=0, tiled=True),
        lax.all_gather(key_weight, "wide", axis=0, tiled=True),
        lax.all_gather(value_weight, "wide", axis=0, tiled=True),
    )
    query, keys, values = tuple(
        (jnp.dot(normed, rows_now, preferred_element_type=jnp.float32) for rows_now in weight_rows)
    )
    head_shape = (groups * slab_frames, site_count, head_count, HEAD_DIM)
    query_heads = query.astype(jnp.bfloat16).reshape(head_shape)
    key_heads = keys.astype(jnp.bfloat16).reshape(head_shape)
    value_heads = values.astype(jnp.bfloat16).reshape(head_shape)
    scores = (
        jnp.einsum("bshd,buhd->bhsu", query_heads, key_heads, preferred_element_type=jnp.float32)
        * scale
    )
    key_limit = jnp.repeat(key_tokens, slab_frames)
    key_mask = site_pos[None, :] < key_limit[:, None]
    scores = jnp.where(key_mask[:, None, None, :], scores, masked_score)
    top = jnp.max(scores, axis=-1, keepdims=True)
    weights = jnp.exp(scores - top)
    probs = weights / jnp.sum(weights, axis=-1, keepdims=True)
    probs_low = probs.astype(jnp.bfloat16)
    attended = jnp.einsum(
        "bhsu,buhd->bshd", probs_low, value_heads, preferred_element_type=jnp.float32
    ).astype(jnp.bfloat16)
    attended = attended.reshape(-1, model_width)
    output_full = lax.all_gather(output_weight, "wide", axis=0, tiled=True)
    projected = jnp.dot(attended, output_full, preferred_element_type=jnp.float32)
    block = (tokens.astype(jnp.float32) + projected).astype(jnp.bfloat16)
    block = jnp.where(live_rows[:, None], block, jnp.zeros((), jnp.bfloat16))
    block_out = block.reshape(1, groups, slab_frames, site_count, model_width)
    upstream = jnp.where(
        live_rows[:, None], out_grad.reshape(-1, model_width), jnp.zeros((), jnp.bfloat16)
    )
    term_output = jnp.einsum("rk,rd->kd", attended, upstream, preferred_element_type=jnp.float32)
    d_attended = jnp.einsum(
        "rd,kd->rk", upstream, output_full, preferred_element_type=jnp.float32
    ).astype(jnp.bfloat16)
    d_att_heads = d_attended.reshape(head_shape)
    d_probs = jnp.einsum(
        "bshd,buhd->bhsu", d_att_heads, value_heads, preferred_element_type=jnp.float32
    )
    inner = jnp.sum(probs * d_probs, axis=-1, keepdims=True)
    d_scores = (probs * (d_probs - inner) * scale).astype(jnp.bfloat16)
    d_query = (
        jnp.einsum("bhsu,buhd->bshd", d_scores, key_heads, preferred_element_type=jnp.float32)
        .astype(jnp.bfloat16)
        .reshape(-1, model_width)
    )
    d_keys = (
        jnp.einsum("bhsu,bshd->buhd", d_scores, query_heads, preferred_element_type=jnp.float32)
        .astype(jnp.bfloat16)
        .reshape(-1, model_width)
    )
    d_values = (
        jnp.einsum("bhsu,bshd->buhd", probs_low, d_att_heads, preferred_element_type=jnp.float32)
        .astype(jnp.bfloat16)
        .reshape(-1, model_width)
    )
    term_query = jnp.einsum("rk,rd->kd", normed, d_query, preferred_element_type=jnp.float32)
    term_key = jnp.einsum("rk,rd->kd", normed, d_keys, preferred_element_type=jnp.float32)
    term_value = jnp.einsum("rk,rd->kd", normed, d_values, preferred_element_type=jnp.float32)
    shares = (
        lax.psum_scatter(
            term_query.astype(jnp.bfloat16), "wide", scatter_dimension=0, tiled=True
        ).astype(jnp.float32),
        lax.psum_scatter(
            term_key.astype(jnp.bfloat16), "wide", scatter_dimension=0, tiled=True
        ).astype(jnp.float32),
        lax.psum_scatter(
            term_value.astype(jnp.bfloat16), "wide", scatter_dimension=0, tiled=True
        ).astype(jnp.float32),
        lax.psum_scatter(
            term_output.astype(jnp.bfloat16), "wide", scatter_dimension=0, tiled=True
        ).astype(jnp.float32),
    )
    totals = jax.tree.map(
        lambda part: part.astype(jnp.float32), lax.psum(as_sent(tuple(shares)), "dp")
    )
    return (block_out, totals[0], totals[1], totals[2], totals[3])


def solution(mesh):
    in_specs = (
        P("dp", None, "wide", None, None),
        P(),
        P(),
        P("wide", None),
        P("wide", None),
        P("wide", None),
        P("wide", None),
        P("dp", None, "wide", None, None),
        P(),
        P(),
        P(),
        P(),
    )
    out_specs = (
        P("dp", None, "wide", None, None),
        P("wide", None),
        P("wide", None),
        P("wide", None),
        P("wide", None),
    )
    return jax.shard_map(body, mesh=mesh, in_specs=in_specs, out_specs=out_specs, check_vma=False)
```

profile of v0, /device:TPU:0, one launch (start us, length us, event | category | flops | bytes accessed | tf_op | source)
XLA Modules:
  0.0 827.6 jit_solution(10473469134186979574)
XLA Ops:
  7.3 0.7 all-gather.5.cloned.1.call-update
  8.0 0.7 all-gather.9.cloned.1.call-update
  8.8 0.7 all-gather.7.cloned.1.call-update
  9.5 0.5 all-gather.11.cloned.1.call-update
  10.0 4.9 collective-permute-start
  15.0 0.2 select_reduce_fusion
  15.2 0.1 select_reduce_fusion.2
  15.5 5.0 collective-permute-done
  20.5 1.4 convolution_add_fusion.3
  21.9 0.3 convolution_add_fusion.2
  22.2 0.3 fusion.43
  22.6 0.6 convolution_convert_fusion.9
  23.2 1.6 convolution_convert_fusion.8
  24.7 1.4 copy.95
  26.1 3.7 all-to-all-start
  29.8 0.2 reduce-scatter.5.cloned.1.call-start
  30.5 1.5 bitcast_select_fusion
  31.9 17.9 %all-to-all-done = bf16[4,2,64,1536]{3,2,1,0:T(8,128)(2,1)S(1)} async-done(((bf16[4,2,64,1536]{3,2,1,0:T(8,128)(2,1)}), bf16[4,2,64,1536]{3,2,1,0:T(8,128)(2,1)S(1)}, u32[]{:S(2)}, u32[]{:S(2)}) %all-to-all-start) | async-done | bytes 1572896 | tf_op jit(solution)/shard_map/all_to_all | solution.py:87
  49.9 0.3 convert_reduce_fusion
  50.2 0.6 multiply_reduce_fusion.1
  50.9 1.6 fusion.3
  52.5 1.7 multiply_convert_fusion.1
  54.2 38.1 %all-gather.5.cloned.1.call-done = bf16[1536,1536]{1,0:T(8,128)(2,1)} async-done(((bf16[192,1536]{1,0:T(8,128)(2,1)}), bf16[1536,1536]{1,0:T(8,128)(2,1)}) %all-gather.5.cloned.1.call-update) | async-done | bytes 4718608 | tf_op jit(solution)/shard_map/all_gather | solution.py:100
  92.3 6.6 convolution_convert_fusion.7
  98.9 4.0 reshape.240
  102.9 69.3 %all-gather.9.cloned.1.call-done = bf16[1536,1536]{1,0:T(8,128)(2,1)} async-done(((bf16[192,1536]{1,0:T(8,128)(2,1)}), bf16[1536,1536]{1,0:T(8,128)(2,1)}) %all-gather.9.cloned.1.call-update) | async-done | bytes 4718608 | tf_op jit(solution)/shard_map/all_gather | solution.py:99
  172.2 6.6 convolution_convert_fusion.5
  178.8 4.0 reshape.242
  182.8 69.3 %all-gather.7.cloned.1.call-done = bf16[1536,1536]{1,0:T(8,128)(2,1)} async-done(((bf16[192,1536]{1,0:T(8,128)(2,1)}), bf16[1536,1536]{1,0:T(8,128)(2,1)}) %all-gather.7.cloned.1.call-update) | async-done | bytes 4718608 | tf_op jit(solution)/shard_map/all_gather | solution.py:98
  252.1 6.6 convolution_convert_fusion.6
  258.7 4.0 reshape.241
  262.7 69.2 %all-gather.11.cloned.1.call-done = bf16[1536,1536]{1,0:T(8,128)(2,1)} async-done(((bf16[192,1536]{1,0:T(8,128)(2,1)}), bf16[1536,1536]{1,0:T(8,128)(2,1)}) %all-gather.11.cloned.1.call-update) | async-done | bytes 4718608 | tf_op jit(solution)/shard_map/all_gather | solution.py:124
  331.9 6.6 convolution_convert_fusion.4
  338.5 4.0 reshape.246
  342.4 3.2 fusion.52
  345.6 3.1 fusion.84
  348.8 2.6 fusion.47
  351.4 7.8 fusion.40
  359.2 2.6 copy.113
  361.8 4.7 convolution_convert_fusion.3
  366.5 8.0 fusion.37
  374.5 2.6 copy.115
  377.1 4.6 convolution_convert_fusion.2
  381.8 0.3 reduce-scatter.9.cloned.1.call-start
  382.1 3.2 fusion.36
  385.3 1.1 copy.117
  386.4 0.3 copy-done.9
  386.7 4.7 convolution_convert_fusion.1
  391.5 0.2 broadcast_select_fusion
  391.7 1.5 copy-done.3
  393.2 2.9 fusion.35
  396.1 1.1 copy.107
  397.2 1.4 copy-done.6
  398.6 4.5 convolution_convert_fusion
  403.2 57.5 %reduce-scatter.5.cloned.1.call-done = bf16[192,1536]{1,0:T(8,128)(2,1)} async-done(((bf16[1536,1536]{1,0:T(8,128)(2,1)}), bf16[192,1536]{1,0:T(8,128)(2,1)}) %reduce-scatter.5.cloned.1.call-update) | async-done | bytes 589840 | tf_op jit(solution)/shard_map/reduce_scatter | solution.py:161
  460.6 98.8 %reduce-scatter.7.cloned.1.call-done = bf16[192,1536]{1,0:T(8,128)(2,1)} async-done(((bf16[1536,1536]{1,0:T(8,128)(2,1)}), bf16[192,1536]{1,0:T(8,128)(2,1)}) %reduce-scatter.7.cloned.1.call-update) | async-done | bytes 589840 | tf_op jit(solution)/shard_map/reduce_scatter | solution.py:164
  559.4 99.0 %reduce-scatter.9.cloned.1.call-done = bf16[192,1536]{1,0:T(8,128)(2,1)} async-done(((bf16[1536,1536]{1,0:T(8,128)(2,1)}), bf16[192,1536]{1,0:T(8,128)(2,1)}) %reduce-scatter.9.cloned.1.call-update) | async-done | bytes 589840 | tf_op jit(solution)/shard_map/reduce_scatter | solution.py:167
  658.4 99.0 %reduce-scatter.11.cloned.1.call-done = bf16[192,1536]{1,0:T(8,128)(2,1)} async-done(((bf16[1536,1536]{1,0:T(8,128)(2,1)}), bf16[192,1536]{1,0:T(8,128)(2,1)}) %reduce-scatter.11.cloned.1.call-update) | async-done | bytes 589840 | tf_op jit(solution)/shard_map/reduce_scatter | solution.py:170
  757.4 6.7 fusion.6
  764.1 51.2 %all-reduce.3.cloned.1.call-done = (bf16[192,1536]{1,0:T(8,128)(2,1)}, bf16[192,1536]{1,0:T(8,128)(2,1)}, bf16[192,1536]{1,0:T(8,128)(2,1)}, bf16[192,1536]{1,0:T(8,128)(2,1)}) async-done(((bf16[192,1536]{1,0:T(8,128)(2,1)}, bf16[192,1536]{1,0:T(8,128)(2,1)}, bf16[192,1536]{1,0:T(8,128)(2,1)}, bf16[192,1536]{1,0:T(8,128)(2,1)}), (bf16[192,1536]{1,0:T(8,128)(2,1)}, bf16[192,1536]{1,0:T(8,128)(2,1)}, ...) | async-done | bytes 2359312 | tf_op jit(solution)/shard_map/psum | solution.py:175
  815.3 2.3 convert_element_type.154
  817.6 1.1 convert_element_type.158
  818.8 1.1 convert_element_type.162
  819.9 1.1 convert_element_type.164
  (64 shorter events, 1.2 us)
Async XLA Ops:
  7.2 15.4 %copy-start = (bf16[512,1536]{1,0:T(8,128)(2,1)S(1)}, bf16[512,1536]{1,0:T(8,128)(2,1)}, u32[]{:S(2)}) copy-start(bf16[512,1536]{1,0:T(8,128)(2,1)} %param.14) | copy-start | bytes 4718596
  7.2 2.8 copy-start.18
  7.2 7.8 copy-start.16
  7.2 7.8 copy-start.14
  7.2 8.0 copy-start.13
  7.2 8.0 copy-start.15
  7.2 85.1 %all-gather.5.cloned.1.call-start = ((), (), s32[]{:S(2)}) async-start(), calls=%async_computation.5 | async-start | bytes 5308416 | tf_op jit(solution)/shard_map/all_gather | solution.py:100
  8.0 164.2 %all-gather.9.cloned.1.call-start = ((), (), s32[]{:S(2)}) async-start(), calls=%async_computation.7 | async-start | bytes 5308416 | tf_op jit(solution)/shard_map/all_gather | solution.py:99
  8.7 243.4 %all-gather.7.cloned.1.call-start = ((), (), s32[]{:S(2)}) async-start(), calls=%async_computation.6 | async-start | bytes 5308416 | tf_op jit(solution)/shard_map/all_gather | solution.py:98
  9.5 322.4 %all-gather.11.cloned.1.call-start = ((), (), s32[]{:S(2)}) async-start(), calls=%async_computation.8 | async-start | bytes 5308416 | tf_op jit(solution)/shard_map/all_gather | solution.py:124
  10.0 10.4 %collective-permute-start = (bf16[2,2,64,512]{3,2,1,0:T(8,128)(2,1)S(1)}, bf16[2,2,64,512]{3,2,1,0:T(8,128)(2,1)S(1)}, u32[]{:S(2)}, u32[]{:S(2)}) collective-permute-start(bf16[2,2,64,512]{3,2,1,0:T(8,128)(2,1)S(1)} %bitcast.101), channel_id=1, source_target_pairs={{0,1},{1,2},{2,3},{3,4},{4,5},{5,6},{6,7},{8,9},{9,10},{10,11},{11... | collective-permute-start | bytes 786440 | tf_op jit(solution)/shard_map/ppermute | solution.py:18
  15.5 6.4 copy-start.17
  26.1 4.3 copy-start.5
  26.1 23.7 %all-to-all-start = ((bf16[4,2,64,1536]{3,2,1,0:T(8,128)(2,1)}), bf16[4,2,64,1536]{3,2,1,0:T(8,128)(2,1)S(1)}, u32[]{:S(2)}, u32[]{:S(2)}) async-start(bf16[4,2,64,1536]{3,2,1,0:T(8,128)(2,1)} %copy.95), calls=%async_computation | async-start | bytes 3145728 | tf_op jit(solution)/shard_map/all_to_all | solution.py:87
  29.8 430.8 %reduce-scatter.5.cloned.1.call-start = ((), (), s32[]{:S(2)}) async-start(), calls=%async_computation.9 | async-start | bytes 5308416 | tf_op jit(solution)/shard_map/reduce_scatter | solution.py:161
  345.6 3.1 copy-start.2
  345.6 3.1 copy-start.4
  359.2 2.6 copy-start.7
  366.5 193.0 %reduce-scatter.7.cloned.1.call-start = ((), (), s32[]{:S(2)}) async-start(), calls=%async_computation.10 | async-start | bytes 5308416 | tf_op jit(solution)/shard_map/reduce_scatter | solution.py:164
  374.5 2.6 copy-start.8
  381.8 276.6 %reduce-scatter.9.cloned.1.call-start = ((), (), s32[]{:S(2)}) async-start(), calls=%async_computation.11 | async-start | bytes 5308416 | tf_op jit(solution)/shard_map/reduce_scatter | solution.py:167
  385.3 1.4 copy-start.9
  391.4 365.9 %reduce-scatter.11.cloned.1.call-start = ((), (), s32[]{:S(2)}) async-start(), calls=%async_computation.12 | async-start | bytes 5308416 | tf_op jit(solution)/shard_map/reduce_scatter | solution.py:170
  391.5 1.7 copy-start.3
  397.2 1.4 copy-start.6
  403.1 412.2 %all-reduce.3.cloned.1.call-start = ((), (), s32[]{:S(2)}) async-start(), calls=%async_computation.13 | async-start | bytes 4718592 | tf_op jit(solution)/shard_map/psum | solution.py:175
  815.3 2.3 copy-start.12
  815.3 3.5 copy-start.11
  817.6 2.3 copy-start.10
  817.6 3.4 copy-start.1
Sparse Core Ops, SparseCore 0:
  10.2 82.0 all-gather.4
  94.5 77.6 all-gather.8
  174.4 77.6 all-gather.6
  254.2 77.6 all-gather.10
  366.6 94.0 reduce-scatter.4
  464.1 95.2 reduce-scatter.6
  563.1 95.2 reduce-scatter.8
  662.0 95.2 reduce-scatter.10
  759.9 55.3 all-reduce.2
where the time goes:
time: 828 us
  waiting for transfers between devices  677 us (82%)
  matrix products  83.3 us (10%)
  local copies, waits for them, and re-layouts  28.6 us (3%)
  other arithmetic  15.3 us (2%)
  between operations  14.1 us (2%)
  starting transfers between devices  9.38 us (1%)
    reduce_scatter x1, waiting for transfers between devices, body(): lax.psum_scatter(term_value.astype(jnp.bfloat16), 'wide', scatter_dimensi...  99 us
    reduce_scatter x1, waiting for transfers between devices, body(): lax.psum_scatter(term_output.astype(jnp.bfloat16), 'wide', scatter_dimens...  99 us
    reduce_scatter x1, waiting for transfers between devices, body(): lax.psum_scatter(term_key.astype(jnp.bfloat16), 'wide', scatter_dimension...  98.8 us
    all_gather x1, waiting for transfers between devices, body(): lax.all_gather(query_weight, 'wide', axis=0, tiled=True)  69.3 us
    all_gather x1, waiting for transfers between devices, body(): lax.all_gather(key_weight, 'wide', axis=0, tiled=True)  69.3 us
    all_gather x1, waiting for transfers between devices, body(): output_full = lax.all_gather(output_weight, 'wide', axis=0, tiled=True)  69.2 us
    reduce_scatter x1, waiting for transfers between devices, body(): lax.psum_scatter(term_query.astype(jnp.bfloat16), 'wide', scatter_dimensi...  57.5 us
    psum x1, waiting for transfers between devices, body(): lax.psum(as_sent(tuple(shares)), 'dp')  51.2 us
  transfers between devices with their start and end apart: 11, of which 11 were waited for; matrix products, arithmetic and copies ran while one was open for 10% of the time, Pallas kernels for 0%

commit v1 on v0

--- a/solution.py
+++ b/solution.py
@@ -1,11 +1,16 @@
+import functools
 import math
 
 import jax
 import jax.numpy as jnp
 from jax import lax
+from jax.experimental import pallas as pl
+from jax.experimental.pallas import tpu as pltpu
 from jax.sharding import PartitionSpec as P
 
 HEAD_DIM = 128
+CORES = 2
+MESH = pl.DeviceIdType.MESH
 
 
 EPS = 1e-06
@@ -16,10 +21,6 @@
     count = lax.axis_size(axis)
     pairs = [(i, i + by) for i in range(count) if 0 <= i + by < count]
     return lax.ppermute(shard, axis, pairs)
-
-
-def as_sent(shard):
-    return jax.tree.map(lambda a: a.astype(jnp.bfloat16) if a.dtype == jnp.float32 else a, shard)
 
 
 def layer_norm(values):
@@ -27,6 +28,305 @@
     center = floats - jnp.mean(floats, axis=-1, keepdims=True)
     spread = jnp.mean(center * center, axis=-1, keepdims=True)
     return (center * lax.rsqrt(spread + EPS)).astype(jnp.bfloat16)
+
+
+class Place:
+    def __init__(self, n_wide):
+        self.dp = lax.axis_index("dp")
+        self.wide = lax.axis_index("wide")
+        self.plane, self.core = self.dp // CORES, self.dp % CORES
+        self.level, self.side = self.wide // 2, self.wide % 2
+        self.levels = n_wide // 2
+        self.sibling = (self.plane * CORES + 1 - self.core, self.wide)
+        self.across = ((1 - self.plane) * CORES + self.core, self.wide)
+        self.beside = (self.dp, self.level * 2 + 1 - self.side)
+
+    def level_at(self, offset):
+        return lax.rem(self.level + offset, self.levels)
+
+    def above(self, offset):
+        return (self.dp, self.level_at(offset) * 2 + self.side)
+
+    def greet(self):
+        barrier = pltpu.get_barrier_semaphore()
+        peers = [self.sibling, self.across, self.beside]
+        peers += [self.above(o) for o in range(1, self.levels)]
+        for peer in peers:
+            pl.semaphore_signal(barrier, inc=1, device_id=peer, device_id_type=MESH)
+        pl.semaphore_wait(barrier, len(peers))
+
+
+def span(start, size):
+    return pl.ds(pl.multiple_of(start, size), size)
+
+
+def remote(src, dst, send, recv, peer):
+    return pltpu.make_async_remote_copy(
+        src_ref=src, dst_ref=dst, send_sem=send, recv_sem=recv, device_id=peer, device_id_type=MESH
+    )
+
+
+def gather_kernel(n_wide, count, *refs):
+    shards, fulls = refs[:count], refs[count : 2 * count]
+    local_sem, flat_send, flat_recv, across_send, across_recv, core_send, core_recv = refs[2 * count :]
+    here = Place(n_wide)
+    rows, width = shards[0].shape
+    third = width // (CORES * 3)
+    half = here.core * (3 * third)
+    flat_cols = pl.ds(pl.multiple_of(half + here.plane * third, third), 2 * third)
+    across_cols = pl.ds(pl.multiple_of(half + here.plane * (2 * third), third), third)
+    core_cols = pl.ds(pl.multiple_of(half, third), 3 * third)
+    levels = here.levels
+
+    def block(offset, other):
+        side = 1 - here.side if other else here.side
+        return pl.ds(pl.multiple_of((here.level_at(offset) * 2 + side) * rows, rows), rows)
+
+    here.greet()
+    pending = []
+    own = block(0, 0)
+    for k in range(count):
+        for offset in range(0, levels):
+            peer = here.above(offset) if offset else here.beside
+            slot = (k, levels - offset, 0) if offset else (k, 0, 1)
+            copy = remote(
+                shards[k].at[:, flat_cols],
+                fulls[k].at[own, flat_cols],
+                flat_send.at[k, 0, offset],
+                flat_recv.at[slot],
+                peer,
+            )
+            copy.start()
+            pending.append(copy)
+    locals_ = []
+    for k in range(count):
+        copy = pltpu.make_async_copy(shards[k], fulls[k].at[own, :], local_sem.at[k])
+        copy.start()
+        locals_.append(copy)
+
+    def arrived(k, where, cols, recv):
+        view = fulls[k].at[where, cols]
+        remote(view, view, local_sem.at[k], recv, here.sibling).wait_recv()
+
+    def finish_core(k):
+        for other in range(2):
+            for offset in range(1 - other, levels):
+                where = block(offset, other)
+                peer_cols = pl.ds(
+                    pl.multiple_of(half + (1 - here.plane) * (2 * third), third), third
+                )
+                arrived(k, where, peer_cols, across_recv.at[k, offset, other])
+                view = fulls[k].at[where, core_cols]
+                copy = remote(
+                    view, view, core_send.at[k, offset, other], core_recv.at[k, offset, other], here.sibling
+                )
+                copy.start()
+                pending.append(copy)
+
+    for k in range(count):
+        for other in range(2):
+            for offset in range(1 - other, levels):
+                where = block(offset, other)
+                arrived(k, where, flat_cols, flat_recv.at[k, offset, other])
+                if not other:
+                    view = fulls[k].at[where, flat_cols]
+                    copy = remote(
+                        view, view, flat_send.at[k, 1, offset], flat_recv.at[k, offset, 1], here.beside
+                    )
+                    copy.start()
+                    pending.append(copy)
+                view = fulls[k].at[where, across_cols]
+                copy = remote(
+                    view, view, across_send.at[k, offset, other], across_recv.at[k, offset, other], here.across
+                )
+                copy.start()
+                pending.append(copy)
+        if k:
+            finish_core(k - 1)
+    finish_core(count - 1)
+    sibling_cols = pl.ds(pl.multiple_of((1 - here.core) * (3 * third), third), 3 * third)
+    for k in range(count):
+        for other in range(2):
+            for offset in range(1 - other, levels):
+                arrived(k, block(offset, other), sibling_cols, core_recv.at[k, offset, other])
+    for copy in locals_:
+        copy.wait()
+    for copy in pending:
+        copy.wait_send()
+
+
+def gather_weights(n_wide, *shards):
+    count = len(shards)
+    rows, width = shards[0].shape
+    levels = n_wide // 2
+    dma = pltpu.SemaphoreType.DMA
+    return pl.pallas_call(
+        functools.partial(gather_kernel, n_wide, count),
+        out_shape=[jax.ShapeDtypeStruct((n_wide * rows, width), s.dtype) for s in shards],
+        in_specs=[pl.BlockSpec(memory_space=pltpu.VMEM)] * count,
+        out_specs=[pl.BlockSpec(memory_space=pl.ANY)] * count,
+        scratch_shapes=[
+            dma((count,)),
+            dma((count, 2, levels)),
+            dma((count, levels, 2)),
+            dma((count, levels, 2)),
+            dma((count, levels, 2)),
+            dma((count, levels, 2)),
+            dma((count, levels, 2)),
+        ],
+        compiler_params=pltpu.CompilerParams(
+            collective_id=0, has_side_effects=True, vmem_limit_bytes=16 * 1024 * 1024
+        ),
+        name="gather_weights",
+    )(*shards)
+
+
+def sum_kernel(n_wide, count, *refs):
+    terms, out = refs[:count], refs[count]
+    half_buf, third_buf, side_buf, level_buf, pair_out, pair_in, fin_out, fin_in = refs[count + 1 : count + 9]
+    core_s, core_r, across_s, across_r, side_s, side_r, level_s, level_r, pair_s, pair_r, fin_s, fin_r = refs[
+        count + 9 :
+    ]
+    here = Place(n_wide)
+    levels, _, rows, width = terms[0].shape
+    third = width // (CORES * 3)
+    f32, bf16 = jnp.float32, jnp.bfloat16
+
+    def cols(start, size):
+        return pl.ds(pl.multiple_of(start, third), size)
+
+    mine = cols(here.core * (3 * third), 3 * third)
+    theirs = cols((1 - here.core) * (3 * third), 3 * third)
+    flat = cols(here.plane * third, 2 * third)
+    keep = cols(here.plane * (2 * third), third)
+    give = cols((1 - here.plane) * (2 * third), third)
+    here.greet()
+
+    core_copies = []
+    for k in range(count):
+        copy = remote(terms[k].at[:, :, :, theirs], half_buf.at[k], core_s.at[k], core_r.at[k], here.sibling)
+        copy.start()
+        core_copies.append(copy)
+    across_copies, side_copies, level_copies, pair_copies, fin_copies = {}, {}, {}, {}, {}
+
+    def stage_core(k):
+        core_copies[k].wait_recv()
+
+        @pl.loop(0, levels * 2)
+        def _(i):
+            a, b = i // 2, i % 2
+            half_buf[k, a, b] = (
+                half_buf[k, a, b].astype(f32) + terms[k][a, b, :, mine].astype(f32)
+            ).astype(bf16)
+
+        across_copies[k] = remote(
+            half_buf.at[k, :, :, :, give], third_buf.at[k], across_s.at[k], across_r.at[k], here.across
+        )
+        across_copies[k].start()
+
+    def stage_across(k):
+        across_copies[k].wait_recv()
+
+        @pl.loop(0, levels * 2)
+        def _(i):
+            a, b = i // 2, i % 2
+            half_buf[k, a, b, :, keep] = (
+                half_buf[k, a, b, :, keep].astype(f32) + third_buf[k, a, b].astype(f32)
+            ).astype(bf16)
+
+        side_copies[k] = remote(
+            half_buf.at[k, :, 1 - here.side, :, flat], side_buf.at[k], side_s.at[k], side_r.at[k], here.beside
+        )
+        side_copies[k].start()
+
+    def stage_side(k):
+        side_copies[k].wait_recv()
+
+        @pl.loop(0, levels)
+        def _(a):
+            side_buf[k, a] = (
+                side_buf[k, a].astype(f32) + half_buf[k, a, here.side, :, flat].astype(f32)
+            ).astype(bf16)
+
+        level_copies[k] = []
+        for offset in range(1, levels):
+            copy = remote(
+                side_buf.at[k, here.level_at(offset)],
+                level_buf.at[k, offset - 1],
+                level_s.at[k, offset - 1],
+                level_r.at[k, offset - 1],
+                here.above(offset),
+            )
+            copy.start()
+            level_copies[k].append(copy)
+
+    def stage_level(k):
+        total = side_buf[k, here.level].astype(f32)
+        for offset in range(1, levels):
+            level_copies[k][offset - 1].wait_recv()
+            total = total + level_buf[k, offset - 1].astype(f32)
+        pair_out[k] = total.astype(bf16)
+        pair_copies[k] = remote(pair_out.at[k], pair_in.at[k], pair_s.at[k], pair_r.at[k], here.across)
+        pair_copies[k].start()
+
+    def stage_pair(k):
+        pair_copies[k].wait_recv()
+        first, second = cols(0, third), cols(third, third)
+        shared_mine = cols((1 - here.plane) * third, third)
+        shared_peer = cols(here.plane * third, third)
+        shared = pair_out[k, :, shared_mine].astype(f32) + pair_in[k, :, shared_peer].astype(f32)
+        fin_out[k, :, second] = shared.astype(bf16)
+        fin_out[k, :, keep] = pair_out[k, :, cols(here.plane * third, third)]
+        fin_out[k, :, give] = pair_in[k, :, cols((1 - here.plane) * third, third)]
+        fin_copies[k] = remote(fin_out.at[k], fin_in.at[k], fin_s.at[k], fin_r.at[k], here.sibling)
+        fin_copies[k].start()
+        out[k, :, mine] = fin_out[k].astype(f32)
+
+    def stage_fin(k):
+        fin_copies[k].wait_recv()
+        out[k, :, theirs] = fin_in[k].astype(f32)
+
+    stages = (stage_core, stage_across, stage_side, stage_level, stage_pair, stage_fin)
+    for step in range(count + len(stages) - 1):
+        for i, stage in enumerate(stages):
+            if 0 <= step - i < count:
+                stage(step - i)
+    for k in range(count):
+        for copy in (core_copies[k], across_copies[k], side_copies[k], *level_copies[k], pair_copies[k], fin_copies[k]):
+            copy.wait_send()
+
+
+def sum_terms(n_wide, *terms):
+    count = len(terms)
+    width = terms[0].shape[-1]
+    rows = terms[0].shape[0] // n_wide
+    levels = n_wide // 2
+    third = width // (CORES * 3)
+    dma = pltpu.SemaphoreType.DMA
+    bf16 = jnp.bfloat16
+    return pl.pallas_call(
+        functools.partial(sum_kernel, n_wide, count),
+        out_shape=jax.ShapeDtypeStruct((count, rows, width), jnp.float32),
+        in_specs=[pl.BlockSpec(memory_space=pltpu.VMEM)] * count,
+        out_specs=pl.BlockSpec(memory_space=pltpu.VMEM),
+        scratch_shapes=[
+            pltpu.VMEM((count, levels, 2, rows, 3 * third), bf16),
+            pltpu.VMEM((count, levels, 2, rows, third), bf16),
+            pltpu.VMEM((count, levels, rows, 2 * third), bf16),
+            pltpu.VMEM((count, levels - 1, rows, 2 * third), bf16),
+            pltpu.VMEM((count, rows, 2 * third), bf16),
+            pltpu.VMEM((count, rows, 2 * third), bf16),
+            pltpu.VMEM((count, rows, 3 * third), bf16),
+            pltpu.VMEM((count, rows, 3 * third), bf16),
+            *([dma((count,))] * 6),
+            *([dma((count, levels - 1))] * 2),
+            *([dma((count,))] * 4),
+        ],
+        compiler_params=pltpu.CompilerParams(
+            collective_id=1, has_side_effects=True, vmem_limit_bytes=60 * 1024 * 1024
+        ),
+        name="sum_terms",
+    )(*[t.reshape(levels, 2, rows, width) for t in terms])
 
 
 def body(
@@ -69,10 +369,9 @@
     mine = (group_index == my_group).astype(jnp.int32)
     my_owners = jnp.sum(mine[:, None] * owners, axis=0)
     send_table = (my_owners[None, :] == group_index[:, None]).astype(jnp.bfloat16)
-    recv_table = (owners == my_group).astype(jnp.int32)
     grid_tokens = clip_grid[..., 0] * clip_grid[..., 1]
-    live_frames = jnp.sum(recv_table * clip_frames, axis=1)
-    live_tokens = jnp.sum(recv_table * grid_tokens, axis=1)
+    live_frames = jnp.sum(mine[:, None] * clip_frames, axis=0)
+    live_tokens = jnp.sum(mine[:, None] * grid_tokens, axis=0)
     key_tokens = jnp.where(live_tokens > 0, live_tokens, site_count)
     frame_pos = my_slab * slab_frames + jnp.arange(slab_frames, dtype=jnp.int32)
     site_pos = jnp.arange(site_count, dtype=jnp.int32)
@@ -80,29 +379,23 @@
         site_pos[None, None, :] < live_tokens[:, None, None]
     )
     live_rows = live.reshape(-1)
-    embedded = jnp.dot(
+    routed_grad = lax.all_to_all(out_grad[0], "dp", split_axis=0, concat_axis=0, tiled=True)
+    clip_grad = jnp.stack(
+        [lax.dynamic_index_in_dim(routed_grad, my_owners[c], 0, keepdims=False) for c in range(clip_count)]
+    )
+    tokens = jnp.dot(
         encoded.reshape(-1, channels), embed_weight, preferred_element_type=jnp.float32
     ).astype(jnp.bfloat16)
-    embedded = embedded.reshape(clip_count, slab_frames, site_count, model_width)
-    tokens = lax.all_to_all(
-        jnp.einsum(
-            "oc,cfsw->ofsw", send_table, embedded, preferred_element_type=jnp.float32
-        ).astype(jnp.bfloat16),
-        "dp",
-        split_axis=0,
-        concat_axis=0,
-        tiled=True,
-    ).reshape(-1, model_width)
     normed = layer_norm(tokens)
-    weight_rows = (
-        lax.all_gather(query_weight, "wide", axis=0, tiled=True),
-        lax.all_gather(key_weight, "wide", axis=0, tiled=True),
-        lax.all_gather(value_weight, "wide", axis=0, tiled=True),
-    )
+    n_wide = lax.axis_size("wide")
+    query_full, key_full, value_full, output_full = gather_weights(
+        n_wide, query_weight, key_weight, value_weight, output_weight
+    )
+    weight_rows = (query_full, key_full, value_full)
     query, keys, values = tuple(
         (jnp.dot(normed, rows_now, preferred_element_type=jnp.float32) for rows_now in weight_rows)
     )
-    head_shape = (groups * slab_frames, site_count, head_count, HEAD_DIM)
+    head_shape = (clip_count * slab_frames, site_count, head_count, HEAD_DIM)
     query_heads = query.astype(jnp.bfloat16).reshape(head_shape)
     key_heads = keys.astype(jnp.bfloat16).reshape(head_shape)
     value_heads = values.astype(jnp.bfloat16).reshape(head_shape)
@@ -121,13 +414,23 @@
         "bhsu,buhd->bshd", probs_low, value_heads, preferred_element_type=jnp.float32
     ).astype(jnp.bfloat16)
     attended = attended.reshape(-1, model_width)
-    output_full = lax.all_gather(output_weight, "wide", axis=0, tiled=True)
     projected = jnp.dot(attended, output_full, preferred_element_type=jnp.float32)
     block = (tokens.astype(jnp.float32) + projected).astype(jnp.bfloat16)
     block = jnp.where(live_rows[:, None], block, jnp.zeros((), jnp.bfloat16))
-    block_out = block.reshape(1, groups, slab_frames, site_count, model_width)
+    block_out = lax.all_to_all(
+        jnp.einsum(
+            "oc,cfsw->ofsw",
+            send_table,
+            block.reshape(clip_count, slab_frames, site_count, model_width),
+            preferred_element_type=jnp.float32,
+        ).astype(jnp.bfloat16),
+        "dp",
+        split_axis=0,
+        concat_axis=0,
+        tiled=True,
+    )[None]
     upstream = jnp.where(
-        live_rows[:, None], out_grad.reshape(-1, model_width), jnp.zeros((), jnp.bfloat16)
+        live_rows[:, None], clip_grad.reshape(-1, model_width), jnp.zeros((), jnp.bfloat16)
     )
     term_output = jnp.einsum("rk,rd->kd", attended, upstream, preferred_element_type=jnp.float32)
     d_attended = jnp.einsum(
@@ -157,24 +460,11 @@
     term_query = jnp.einsum("rk,rd->kd", normed, d_query, preferred_element_type=jnp.float32)
     term_key = jnp.einsum("rk,rd->kd", normed, d_keys, preferred_element_type=jnp.float32)
     term_value = jnp.einsum("rk,rd->kd", normed, d_values, preferred_element_type=jnp.float32)
-    shares = (
-        lax.psum_scatter(
-            term_query.astype(jnp.bfloat16), "wide", scatter_dimension=0, tiled=True
-        ).astype(jnp.float32),
-        lax.psum_scatter(
-            term_key.astype(jnp.bfloat16), "wide", scatter_dimension=0, tiled=True
-        ).astype(jnp.float32),
-        lax.psum_scatter(
-            term_value.astype(jnp.bfloat16), "wide", scatter_dimension=0, tiled=True
-        ).astype(jnp.float32),
-        lax.psum_scatter(
-            term_output.astype(jnp.bfloat16), "wide", scatter_dimension=0, tiled=True
-        ).astype(jnp.float32),
-    )
-    totals = jax.tree.map(
-        lambda part: part.astype(jnp.float32), lax.psum(as_sent(tuple(shares)), "dp")
-    )
-    return (block_out, totals[0], totals[1], totals[2], totals[3])
+    totals = sum_terms(
+        n_wide,
+        *(t.astype(jnp.bfloat16) for t in (term_value, term_key, term_query, term_output)),
+    )
+    return (block_out, totals[2], totals[1], totals[0], totals[3])
 
 
 def solution(mesh):

time: 828 us -> 330 us (0.40)
  waiting for transfers between devices: 677 us -> 0.01 us
  Pallas kernels: 0 us -> 229 us
  matrix products: 83.3 us -> 51.3 us
  other arithmetic: 15.3 us -> 1.54 us
  between operations: 14.1 us -> 4.95 us
    reduce_scatter x4 -> x0, waiting for transfers between devices: 354 us -> none  [the longest x1 99 us: body(): lax.psum_scatter(term_value.astype(jnp.bfloat16), 'wide', scatter_dimensi...]
    all_gather x4 -> x0, waiting for transfers between devices: 246 us -> none  [the longest x1 69.3 us: body(): lax.all_gather(query_weight, 'wide', axis=0, tiled=True)]
    pallas_call x0 -> x2, Pallas kernels: none -> 229 us  [the longest x1 138 us: sum_terms(): pl.pallas_call(functools.partial(sum_kernel, n_wide, count), out_shape=ja...]
    psum x1 -> x0, waiting for transfers between devices: 51.2 us -> none  [body(): lax.psum(as_sent(tuple(shares)), 'dp')]
    all_to_all x1 -> x2, waiting for transfers between devices: 17.9 us -> 0.01 us  [the longest x1 0.01 us: body(): lax.all_to_all(out_grad[0], 'dp', split_axis=0, concat_axis=0, tiled=True)]
    dot_general x3, matrix products: 19.7 us -> 6.88 us  [body(): jnp.dot(normed, rows_now, preferred_element_type=jnp.float32)]
  transfers between devices with their start and end apart: 11 -> 3, of which waited for: 11 -> 0; matrix products, arithmetic and copies ran while one was open for 10% -> 21% of each run, Pallas kernels for 0% -> 70%
where the time goes in v1:
time: 330 us; the launch traced here: 326 us
  Pallas kernels  229 us (69%)
  matrix products  51.3 us (16%)
  local copies, waits for them, and re-layouts  25 us (8%)
  starting transfers between devices  14 us (4%)
  between operations  4.95 us (2%)
    pallas_call x1, Pallas kernels, sum_terms(): pl.pallas_call(functools.partial(sum_kernel, n_wide, count), out_shape=ja...  138 us
    pallas_call x1, Pallas kernels, gather_weights(): pl.pallas_call(functools.partial(gather_kernel, n_wide, count), out_shape...  91.5 us
    unnamed x51, local copies, waits for them, and re-layouts  8.6 us
    dot_general x3, matrix products, body(): jnp.dot(normed, rows_now, preferred_element_type=jnp.float32)  6.88 us
  transfers between devices with their start and end apart: 3, of which 0 were waited for; matrix products, arithmetic and copies ran while one was open for 21% of the time, Pallas kernels for 70%

profile of v1, /device:TPU:0, one launch (start us, length us, event | category | flops | bytes accessed | tf_op | source)
XLA Modules:
  0.0 325.9 jit_solution(18242312105686618792)
XLA Ops:
  0.6 0.0 copy-start
  0.7 4.6 %all-to-all-start.1 = ((bf16[4,2,64,1536]{3,2,1,0:T(8,128)(2,1)}), bf16[4,2,64,1536]{3,2,1,0:T(8,128)(2,1)}, u32[]{:S(2)}, u32[]{:S(2)}) async-start(bf16[4,2,64,1536]{3,2,1,0:T(8,128)(2,1)} %bitcast.108), calls=%async_computation.1 | async-start | bytes 3145728 | tf_op jit(solution)/shard_map/all_to_all | solution.py:382
  5.3 5.6 %collective-permute-start = (bf16[2,2,64,512]{3,2,1,0:T(8,128)(2,1)}, bf16[2,2,64,512]{3,2,1,0:T(8,128)(2,1)}, u32[]{:S(2)}, u32[]{:S(2)}) collective-permute-start(bf16[2,2,64,512]{3,2,1,0:T(8,128)(2,1)} %bitcast.111), channel_id=1, source_target_pairs={{0,1},{1,2},{2,3},{3,4},{4,5},{5,6},{6,7},{8,9},{9,10},{10,11},{11... | collective-permute-start | bytes 786440 | tf_op jit(solution)/shard_map/ppermute | solution.py:23
  11.0 0.2 select_reduce_fusion
  11.2 0.1 multiply_reduce_fusion.4
  11.4 0.1 iota_compare_fusion.2
  11.4 0.1 broadcast_compare_fusion
  11.5 0.1 broadcast_and_fusion
  11.6 0.6 fusion.80
  14.8 0.1 and.26
  14.9 0.1 broadcast_in_dim.63
  14.9 0.1 lt.69
  16.3 0.0 copy-start.5
  16.3 1.1 copy-done.5
  17.4 91.5 %gather_weights.1 = (bf16[1536,1536]{1,0:T(8,128)(2,1)S(1)}, bf16[1536,1536]{1,0:T(8,128)(2,1)S(1)}, bf16[1536,1536]{1,0:T(8,128)(2,1)S(1)}, bf16[1536,1536]{1,0:T(8,128)(2,1)S(1)}) custom-call(bf16[192,1536]{1,0:T(8,128)(2,1)S(1)} %copy-done.2, bf16[192,1536]{1,0:T(8,128)(2,1)S(1)} %copy-done.3, bf16[192,1536]{1,0:T(8,128)(2,1)S(1)} %copy-done.4, ...), custom_call_target="tpu_custom_call" | custom-call | tf_op jit(solution)/shard_map/gather_weights/pallas_call | solution.py:163
  109.0 2.2 copy-done.7
  111.1 0.1 iota_compare_fusion.1
  111.2 0.3 convolution_add_fusion.3
  111.6 1.7 copy-done.6
  113.3 1.2 convolution_add_fusion.2
  114.5 1.3 fusion.30
  115.8 0.7 fusion.81
  116.5 0.3 multiply_reduce_fusion.1
  116.8 0.2 multiply_convert_fusion.1
  117.0 0.6 copy-done.8
  117.6 1.4 convolution_convert_fusion.9
  119.0 1.4 convolution_convert_fusion.8
  120.4 0.5 reshape.215
  121.0 0.0 copy-start.14
  121.0 4.1 %convolution_convert_fusion.7 = bf16[256,1536]{1,0:T(8,128)(2,1)S(1)} fusion(bf16[256,1536]{1,0:T(8,128)(2,1)S(1)} %multiply_convert_fusion.1, bf16[1536,1536]{1,0:T(8,128)(2,1)} %copy-done.7), kind=kOutput, calls=%fused_computation.12 | convolution fusion | flops 1208352768 | bytes 6291456 | tf_op jit(solution)/shard_map/dot_general | solution.py:396
  125.1 1.5 reshape.216
  126.6 3.2 fusion.82
  129.8 0.5 reshape.214
  130.4 0.0 copy-start.12
  130.4 2.3 fusion.22
  132.7 0.0 copy-start.9
  132.7 0.5 copy.68
  133.3 0.2 slice-done.1
  133.5 0.9 copy-done.9
  134.3 1.4 fusion.4
  135.7 1.5 convolution_convert_fusion.4
  137.3 1.4 copy.70
  138.7 0.0 all-to-all-done.1
  138.7 3.7 %all-to-all-start = ((bf16[4,2,64,1536]{3,2,1,0:T(8,128)(2,1)}), bf16[4,2,64,1536]{3,2,1,0:T(8,128)(2,1)S(1)}, u32[]{:S(2)}, u32[]{:S(2)}) async-start(bf16[4,2,64,1536]{3,2,1,0:T(8,128)(2,1)} %copy.70), calls=%async_computation | async-start | bytes 3145728 | tf_op jit(solution)/shard_map/all_to_all | solution.py:420
  142.4 1.2 constant_dynamic-slice_fusion
  143.6 0.2 broadcast_select_fusion
  143.8 0.2 bitcast_select_fusion
  143.9 4.6 %convolution_convert_fusion.6 = bf16[256,1536]{1,0:T(8,128)(2,1)} fusion(bf16[256,1536]{1,0:T(8,128)(2,1)S(1)} %bitcast_select_fusion, bf16[1536,1536]{1,0:T(8,128)(2,1)} %copy-done.6), kind=kOutput, calls=%fused_computation.11 | convolution fusion | flops 1208352768 | bytes 6291456 | tf_op jit(solution)/shard_map/rd,kd->rk/dot_general | solution.py:436
  148.6 2.4 reshape.220
  151.0 3.2 fusion.48
  154.2 4.9 %fusion.27 = bf16[4,64,12,128]{3,1,2,0:T(8,128)(2,1)} fusion(f32[4,12,64,64]{2,3,1,0:T(8,128)} %fusion.48, bf16[4,64,12,128]{3,2,1,0:T(8,128)(2,1)} %copy-done.14, f32[4,12,64,64]{2,3,1,0:T(8,128)} %get-tuple-element.39, f32[4,12,64]{2,1,0:T(8,128)S(1)} %get-tuple-element.38), kind=kOutput, calls=%fused_computation.35 | convolution fusion | flops 52104256 | bytes 3158016 | tf_op jit(solution)/shard_map/bhsu,bshd->buhd/dot_general | solution.py:451
  159.1 4.8 %fusion.24 = bf16[4,64,12,128]{3,1,2,0:T(8,128)(2,1)} fusion(f32[4,12,64,64]{2,3,1,0:T(8,128)} %fusion.48, bf16[4,64,12,128]{3,2,1,0:T(8,128)(2,1)} %reshape.216, f32[4,12,64,64]{2,3,1,0:T(8,128)} %get-tuple-element.39, f32[4,12,64]{2,1,0:T(8,128)S(1)} %get-tuple-element.38), kind=kOutput, calls=%fused_computation.34 | convolution fusion | flops 52104256 | bytes 3158016 | tf_op jit(solution)/shard_map/bhsu,buhd->bshd/dot_general | solution.py:446
  164.0 1.8 copy.79
  165.8 0.5 copy.76
  166.4 3.7 %convolution_convert_fusion = bf16[1536,1536]{1,0:T(8,128)(2,1)} fusion(bf16[256,1536]{1,0:T(8,128)(2,1)S(1)} %bitcast.107, bf16[32,8,12,128]{3,2,1,0:T(8,128)(2,1)S(1)} %bitcast.103), kind=kOutput, calls=%fused_computation.2 | convolution fusion | flops 1210318848 | bytes 6291456 | tf_op jit(solution)/shard_map/rk,rd->kd/dot_general | solution.py:435
  170.0 3.6 %convolution_convert_fusion.2 = bf16[1536,1536]{1,0:T(8,128)(2,1)} fusion(bf16[256,1536]{1,0:T(8,128)(2,1)S(1)} %multiply_convert_fusion.1, bf16[32,8,12,128]{3,2,1,0:T(8,128)(2,1)S(1)} %bitcast.105), kind=kOutput, calls=%fused_computation.4 | convolution fusion | flops 1210318848 | bytes 6291456 | tf_op jit(solution)/shard_map/rk,rd->kd/dot_general | solution.py:461
  173.6 3.6 %convolution_convert_fusion.1 = bf16[1536,1536]{1,0:T(8,128)(2,1)} fusion(bf16[256,1536]{1,0:T(8,128)(2,1)S(1)} %multiply_convert_fusion.1, bf16[32,8,12,128]{3,2,1,0:T(8,128)(2,1)S(1)} %bitcast.104), kind=kOutput, calls=%fused_computation.3 | convolution fusion | flops 1210318848 | bytes 6291456 | tf_op jit(solution)/shard_map/rk,rd->kd/dot_general | solution.py:460
  177.2 0.4 fusion.23
  177.6 0.5 copy.72
  178.2 3.6 %convolution_convert_fusion.3 = bf16[1536,1536]{1,0:T(8,128)(2,1)} fusion(bf16[256,1536]{1,0:T(8,128)(2,1)S(1)} %multiply_convert_fusion.1, bf16[32,8,12,128]{3,2,1,0:T(8,128)(2,1)S(1)} %bitcast.106), kind=kOutput, calls=%fused_computation.5 | convolution fusion | flops 1210318848 | bytes 6291456 | tf_op jit(solution)/shard_map/rk,rd->kd/dot_general | solution.py:462
  181.7 137.6 %sum_terms.1 = f32[4,192,1536]{2,1,0:T(8,128)} custom-call(bf16[4,2,192,1536]{3,2,1,0:T(8,128)(2,1)} %bitcast.99, bf16[4,2,192,1536]{3,2,1,0:T(8,128)(2,1)} %bitcast.97, bf16[4,2,192,1536]{3,2,1,0:T(8,128)(2,1)} %bitcast.98, bf16[4,2,192,1536]{3,2,1,0:T(8,128)(2,1)} %bitcast.100), custom_call_target="tpu_custom_call" | custom-call | tf_op jit(solution)/shard_map/sum_terms/pallas_call | solution.py:307
  319.3 4.6 %slice_bitcast_fusion = (f32[192,1536]{1,0:T(8,128)}, f32[192,1536]{1,0:T(8,128)}, f32[192,1536]{1,0:T(8,128)}, f32[192,1536]{1,0:T(8,128)}) fusion(f32[4,192,1536]{2,1,0:T(8,128)} %sum_terms.1), kind=kLoop, calls=%fused_computation.40 | loop fusion | bytes 9437184 | tf_op jit(solution)/shard_map/squeeze | solution.py:467
  323.9 1.1 copy.137
  325.0 0.8 copy-done.1
  (47 shorter events, 0.1 us)
Async XLA Ops:
  0.6 115.2 %copy-start = (bf16[512,1536]{1,0:T(8,128)(2,1)S(1)}, bf16[512,1536]{1,0:T(8,128)(2,1)}, u32[]{:S(2)}) copy-start(bf16[512,1536]{1,0:T(8,128)(2,1)} %param.14) | copy-start | bytes 4718596
  0.7 10.3 %copy-start.16 = (s32[4,2,2]{0,2,1:T(2,128)S(1)}, s32[4,2,2]{0,2,1:T(2,128)}, u32[]{:S(2)}) copy-start(s32[4,2,2]{0,2,1:T(2,128)} %param.23) | copy-start | bytes 196
  0.7 10.3 %copy-start.18 = (s32[4,2]{0,1:T(2,128)S(1)}, s32[4,2]{0,1:T(2,128)}, u32[]{:S(2)}) copy-start(s32[4,2]{0,1:T(2,128)} %param.21) | copy-start | bytes 100
  0.7 10.3 %copy-start.19 = (s32[16]{0:T(128)S(1)}, s32[16]{0:T(128)}, u32[]{:S(2)}) copy-start(s32[16]{0:T(128)} %param.20) | copy-start | bytes 196
  0.7 10.5 %copy-start.17 = (s32[4,2]{0,1:T(2,128)S(1)}, s32[4,2]{0,1:T(2,128)}, u32[]{:S(2)}) copy-start(s32[4,2]{0,1:T(2,128)} %param.22) | copy-start | bytes 100
  0.7 15.6 %copy-start.2 = (bf16[192,1536]{1,0:T(8,128)(2,1)S(1)}, bf16[192,1536]{1,0:T(8,128)(2,1)}, u32[]{:S(2)}) copy-start(bf16[192,1536]{1,0:T(8,128)(2,1)} %refs_0_.1) | copy-start | bytes 1769476
  0.7 15.6 %copy-start.3 = (bf16[192,1536]{1,0:T(8,128)(2,1)S(1)}, bf16[192,1536]{1,0:T(8,128)(2,1)}, u32[]{:S(2)}) copy-start(bf16[192,1536]{1,0:T(8,128)(2,1)} %refs_1_.1) | copy-start | bytes 1769476
  0.7 15.6 %copy-start.4 = (bf16[192,1536]{1,0:T(8,128)(2,1)S(1)}, bf16[192,1536]{1,0:T(8,128)(2,1)}, u32[]{:S(2)}) copy-start(bf16[192,1536]{1,0:T(8,128)(2,1)} %refs_2_.1) | copy-start | bytes 1769476
  0.7 138.0 %all-to-all-start.1 = ((bf16[4,2,64,1536]{3,2,1,0:T(8,128)(2,1)}), bf16[4,2,64,1536]{3,2,1,0:T(8,128)(2,1)}, u32[]{:S(2)}, u32[]{:S(2)}) async-start(bf16[4,2,64,1536]{3,2,1,0:T(8,128)(2,1)} %bitcast.108), calls=%async_computation.1 | async-start | bytes 3145728 | tf_op jit(solution)/shard_map/all_to_all | solution.py:382
  5.3 105.9 %collective-permute-start = (bf16[2,2,64,512]{3,2,1,0:T(8,128)(2,1)}, bf16[2,2,64,512]{3,2,1,0:T(8,128)(2,1)}, u32[]{:S(2)}, u32[]{:S(2)}) collective-permute-start(bf16[2,2,64,512]{3,2,1,0:T(8,128)(2,1)} %bitcast.111), channel_id=1, source_target_pairs={{0,1},{1,2},{2,3},{3,4},{4,5},{5,6},{6,7},{8,9},{9,10},{10,11},{11... | collective-permute-start | bytes 786440 | tf_op jit(solution)/shard_map/ppermute | solution.py:23
  16.3 1.1 copy-start.5
  17.4 93.8 %copy-start.20 = (bf16[3,512,512]{2,1,0:T(8,128)(2,1)S(1)}, bf16[3,512,512]{2,1,0:T(8,128)(2,1)}, u32[]{:S(2)}) copy-start(bf16[3,512,512]{2,1,0:T(8,128)(2,1)} %param.13) | copy-start | bytes 4718596
  17.4 93.8 %copy-start.21 = (bf16[1,2,2,64,512]{4,3,2,1,0:T(8,128)(2,1)S(1)}, bf16[1,2,2,64,512]{4,3,2,1,0:T(8,128)(2,1)}, u32[]{:S(2)}) copy-start(bf16[1,2,2,64,512]{4,3,2,1,0:T(8,128)(2,1)} %param.12) | copy-start | bytes 786436
  108.9 2.2 copy-start.7
  111.1 2.1 copy-start.6
  116.5 1.1 copy-start.8
  121.0 5.6 %copy-start.14 = (bf16[4,64,12,128]{3,2,1,0:T(8,128)(2,1)}, bf16[4,64,12,128]{3,2,1,0:T(8,128)(2,1)S(1)}, u32[]{:S(2)}) copy-start(bf16[4,64,12,128]{3,2,1,0:T(8,128)(2,1)S(1)} %reshape.215) | copy-start | bytes 2359300
  129.8 3.5 %slice-start = ((s8[4718592]{0:T(1024)(128)(4,1)}), s8[524288]{0:T(1024)(128)(4,1)S(1)}, s32[]{:S(2)}) async-start(s8[4718592]{0:T(1024)(128)(4,1)} %bitcast.95), calls=%async_computation.2 | async-start | bytes 1048576
  130.4 2.3 copy-start.12
  130.4 3.1 slice-start.1
  132.7 1.6 copy-start.9
  133.3 2.4 copy-start.10
  138.7 185.2 %all-to-all-start = ((bf16[4,2,64,1536]{3,2,1,0:T(8,128)(2,1)}), bf16[4,2,64,1536]{3,2,1,0:T(8,128)(2,1)S(1)}, u32[]{:S(2)}, u32[]{:S(2)}) async-start(bf16[4,2,64,1536]{3,2,1,0:T(8,128)(2,1)} %copy.70), calls=%async_computation | async-start | bytes 3145728 | tf_op jit(solution)/shard_map/all_to_all | solution.py:420
  164.0 1.8 copy-start.15
  164.0 2.4 copy-start.11
  173.6 3.6 %copy-start.13 = (bf16[4,64,12,128]{3,2,1,0:T(8,128)(2,1)S(1)}, bf16[4,64,12,128]{3,2,1,0:T(8,128)(2,1)}, u32[]{:S(2)}) copy-start(bf16[4,64,12,128]{3,2,1,0:T(8,128)(2,1)} %reshape.220) | copy-start | bytes 2359300
  173.6 3.6 %copy-start.22 = (f32[4,12,64,64]{2,3,1,0:T(8,128)S(1)}, f32[4,12,64,64]{2,3,1,0:T(8,128)}, u32[]{:S(2)}) copy-start(f32[4,12,64,64]{2,3,1,0:T(8,128)} %get-tuple-element.39) | copy-start | bytes 2359300
  323.9 2.0 copy-start.1

commit v2 on v1

--- a/solution.py
+++ b/solution.py
@@ -181,16 +181,25 @@
     )(*shards)
 
 
-def sum_kernel(n_wide, count, *refs):
-    terms, out = refs[:count], refs[count]
-    half_buf, third_buf, side_buf, level_buf, pair_out, pair_in, fin_out, fin_in = refs[count + 1 : count + 9]
+def sum_kernel(n_wide, count, parts, site_count, scale, *refs):
+    q_ref, k_ref, v_ref, g_ref, mask_ref, normed_t, attended_t, up_ref = refs[:8]
+    outs = refs[8 : 8 + count]
+    dq_ref, dk_ref, dv_ref = refs[8 + count : 11 + count]
+    send_buf, half_buf, third_buf, side_buf, level_buf, pair_out, pair_in, fin_out, fin_in = refs[
+        11 + count : 20 + count
+    ]
     core_s, core_r, across_s, across_r, side_s, side_r, level_s, level_r, pair_s, pair_r, fin_s, fin_r = refs[
-        count + 9 :
+        20 + count :
     ]
     here = Place(n_wide)
-    levels, _, rows, width = terms[0].shape
+    levels, rows = half_buf.shape[1], half_buf.shape[3]
+    tokens, width = q_ref.shape
+    heads = width // HEAD_DIM
     third = width // (CORES * 3)
     f32, bf16 = jnp.float32, jnp.bfloat16
+    chunks = count * parts
+    left = (attended_t, normed_t, normed_t, normed_t)
+    right = (up_ref, dv_ref, dk_ref, dq_ref)
 
     def cols(start, size):
         return pl.ds(pl.multiple_of(start, third), size)
@@ -202,131 +211,176 @@
     give = cols((1 - here.plane) * (2 * third), third)
     here.greet()
 
-    core_copies = []
-    for k in range(count):
-        copy = remote(terms[k].at[:, :, :, theirs], half_buf.at[k], core_s.at[k], core_r.at[k], here.sibling)
+    def term(c, i, where):
+        k, part = c // parts, c % parts
+        lines = pl.ds(pl.multiple_of(i * (rows * parts) + part * rows, rows), rows)
+        return jnp.dot(left[k][lines, :], right[k][:, where], preferred_element_type=f32)
+
+    def attention(first, last):
+        @pl.loop(first, last)
+        def _(h):
+            lanes = pl.ds(pl.multiple_of(h * HEAD_DIM, HEAD_DIM), HEAD_DIM)
+            for b in range(tokens // site_count):
+                at = pl.ds(b * site_count, site_count)
+                q, k, v, g = q_ref[at, lanes], k_ref[at, lanes], v_ref[at, lanes], g_ref[at, lanes]
+                wide_dot = lambda x, y: lax.dot_general(
+                    x, y, (((1,), (1,)), ((), ())), preferred_element_type=f32
+                )
+                tall_dot = lambda x, y: lax.dot_general(
+                    x, y, (((0,), (0,)), ((), ())), preferred_element_type=f32
+                )
+                scores = jnp.where(mask_ref[pl.ds(b, 1), :] > 0, wide_dot(q, k) * scale, masked_score)
+                weights = jnp.exp(scores - jnp.max(scores, axis=-1, keepdims=True))
+                probs = weights / jnp.sum(weights, axis=-1, keepdims=True)
+                d_probs = wide_dot(g, v)
+                inner = jnp.sum(probs * d_probs, axis=-1, keepdims=True)
+                d_scores = (probs * (d_probs - inner) * scale).astype(bf16)
+                dq_ref[at, lanes] = jnp.dot(d_scores, k, preferred_element_type=f32).astype(bf16)
+                dk_ref[at, lanes] = tall_dot(d_scores, q).astype(bf16)
+                dv_ref[at, lanes] = tall_dot(probs.astype(bf16), g).astype(bf16)
+
+    copies = {}
+
+    def launch(name, c, *args):
+        copy = remote(*args)
         copy.start()
-        core_copies.append(copy)
-    across_copies, side_copies, level_copies, pair_copies, fin_copies = {}, {}, {}, {}, {}
-
-    def stage_core(k):
-        core_copies[k].wait_recv()
-
+        copies.setdefault((name, c), []).append(copy)
+
+    def emit(c):
         @pl.loop(0, levels * 2)
         def _(i):
-            a, b = i // 2, i % 2
-            half_buf[k, a, b] = (
-                half_buf[k, a, b].astype(f32) + terms[k][a, b, :, mine].astype(f32)
-            ).astype(bf16)
-
-        across_copies[k] = remote(
-            half_buf.at[k, :, :, :, give], third_buf.at[k], across_s.at[k], across_r.at[k], here.across
-        )
-        across_copies[k].start()
-
-    def stage_across(k):
-        across_copies[k].wait_recv()
+            send_buf[c, i // 2, i % 2] = term(c, i, theirs).astype(bf16)
+
+        launch("core", c, send_buf.at[c], half_buf.at[c], core_s.at[c], core_r.at[c], here.sibling)
+
+    def stage_core(c):
+        copies["core", c][0].wait_recv()
 
         @pl.loop(0, levels * 2)
         def _(i):
-            a, b = i // 2, i % 2
-            half_buf[k, a, b, :, keep] = (
-                half_buf[k, a, b, :, keep].astype(f32) + third_buf[k, a, b].astype(f32)
+            x, y = i // 2, i % 2
+            half_buf[c, x, y] = (half_buf[c, x, y].astype(f32) + term(c, i, mine)).astype(bf16)
+
+        launch(
+            "across", c, half_buf.at[c, :, :, :, give], third_buf.at[c], across_s.at[c], across_r.at[c], here.across
+        )
+
+    def stage_across(c):
+        copies["across", c][0].wait_recv()
+
+        @pl.loop(0, levels * 2)
+        def _(i):
+            x, y = i // 2, i % 2
+            half_buf[c, x, y, :, keep] = (
+                half_buf[c, x, y, :, keep].astype(f32) + third_buf[c, x, y].astype(f32)
             ).astype(bf16)
 
-        side_copies[k] = remote(
-            half_buf.at[k, :, 1 - here.side, :, flat], side_buf.at[k], side_s.at[k], side_r.at[k], here.beside
+        launch(
+            "side", c, half_buf.at[c, :, 1 - here.side, :, flat], side_buf.at[c], side_s.at[c], side_r.at[c], here.beside
         )
-        side_copies[k].start()
-
-    def stage_side(k):
-        side_copies[k].wait_recv()
+
+    def stage_side(c):
+        copies["side", c][0].wait_recv()
 
         @pl.loop(0, levels)
-        def _(a):
-            side_buf[k, a] = (
-                side_buf[k, a].astype(f32) + half_buf[k, a, here.side, :, flat].astype(f32)
+        def _(x):
+            side_buf[c, x] = (
+                side_buf[c, x].astype(f32) + half_buf[c, x, here.side, :, flat].astype(f32)
             ).astype(bf16)
 
-        level_copies[k] = []
         for offset in range(1, levels):
-            copy = remote(
-                side_buf.at[k, here.level_at(offset)],
-                level_buf.at[k, offset - 1],
-                level_s.at[k, offset - 1],
-                level_r.at[k, offset - 1],
+            launch(
+                "level",
+                c,
+                side_buf.at[c, here.level_at(offset)],
+                level_buf.at[c, offset - 1],
+                level_s.at[c, offset - 1],
+                level_r.at[c, offset - 1],
                 here.above(offset),
             )
-            copy.start()
-            level_copies[k].append(copy)
-
-    def stage_level(k):
-        total = side_buf[k, here.level].astype(f32)
+
+    def stage_level(c):
+        total = side_buf[c, here.level].astype(f32)
         for offset in range(1, levels):
-            level_copies[k][offset - 1].wait_recv()
-            total = total + level_buf[k, offset - 1].astype(f32)
-        pair_out[k] = total.astype(bf16)
-        pair_copies[k] = remote(pair_out.at[k], pair_in.at[k], pair_s.at[k], pair_r.at[k], here.across)
-        pair_copies[k].start()
-
-    def stage_pair(k):
-        pair_copies[k].wait_recv()
-        first, second = cols(0, third), cols(third, third)
+            copies["level", c][offset - 1].wait_recv()
+            total = total + level_buf[c, offset - 1].astype(f32)
+        pair_out[c] = total.astype(bf16)
+        launch("pair", c, pair_out.at[c], pair_in.at[c], pair_s.at[c], pair_r.at[c], here.across)
+
+    def stage_pair(c):
+        copies["pair", c][0].wait_recv()
         shared_mine = cols((1 - here.plane) * third, third)
         shared_peer = cols(here.plane * third, third)
-        shared = pair_out[k, :, shared_mine].astype(f32) + pair_in[k, :, shared_peer].astype(f32)
-        fin_out[k, :, second] = shared.astype(bf16)
-        fin_out[k, :, keep] = pair_out[k, :, cols(here.plane * third, third)]
-        fin_out[k, :, give] = pair_in[k, :, cols((1 - here.plane) * third, third)]
-        fin_copies[k] = remote(fin_out.at[k], fin_in.at[k], fin_s.at[k], fin_r.at[k], here.sibling)
-        fin_copies[k].start()
-        out[k, :, mine] = fin_out[k].astype(f32)
-
-    def stage_fin(k):
-        fin_copies[k].wait_recv()
-        out[k, :, theirs] = fin_in[k].astype(f32)
-
-    stages = (stage_core, stage_across, stage_side, stage_level, stage_pair, stage_fin)
-    for step in range(count + len(stages) - 1):
+        shared = pair_out[c, :, shared_mine].astype(f32) + pair_in[c, :, shared_peer].astype(f32)
+        fin_out[c, :, pl.ds(third, third)] = shared.astype(bf16)
+        fin_out[c, :, keep] = pair_out[c, :, shared_peer]
+        fin_out[c, :, give] = pair_in[c, :, shared_mine]
+        launch("fin", c, fin_out.at[c], fin_in.at[c], fin_s.at[c], fin_r.at[c], here.sibling)
+        outs[c // parts][pl.ds(c % parts * rows, rows), mine] = fin_out[c].astype(f32)
+
+    def stage_fin(c):
+        copies["fin", c][0].wait_recv()
+        outs[c // parts][pl.ds(c % parts * rows, rows), theirs] = fin_in[c].astype(f32)
+
+    for c in range(parts):
+        emit(c)
+    attention(0, heads // 3)
+    stage_core(0)
+    attention(heads // 3, heads * 2 // 3)
+    if parts > 1:
+        stage_core(1)
+    stage_across(0)
+    attention(heads * 2 // 3, heads)
+    done = {(emit, c) for c in range(parts)} | {(stage_core, c) for c in range(parts)} | {(stage_across, 0)}
+    stages = (emit, stage_core, stage_across, stage_side, stage_level, stage_pair, stage_fin)
+    for step in range(chunks + len(stages) - 1):
         for i, stage in enumerate(stages):
-            if 0 <= step - i < count:
-                stage(step - i)
-    for k in range(count):
-        for copy in (core_copies[k], across_copies[k], side_copies[k], *level_copies[k], pair_copies[k], fin_copies[k]):
+            c = step - i
+            if 0 <= c < chunks and (stage, c) not in done:
+                stage(c)
+    for group in copies.values():
+        for copy in group:
             copy.wait_send()
 
 
-def sum_terms(n_wide, *terms):
-    count = len(terms)
-    width = terms[0].shape[-1]
-    rows = terms[0].shape[0] // n_wide
+def sum_terms(n_wide, site_count, scale, q, k, v, d_att, mask, normed_t, attended_t, upstream):
+    count = 4
+    tokens, width = q.shape
+    full_rows = width // n_wide
+    parts = 2 if full_rows % 32 == 0 else 1
+    rows = full_rows // parts
+    chunks = count * parts
     levels = n_wide // 2
     third = width // (CORES * 3)
     dma = pltpu.SemaphoreType.DMA
     bf16 = jnp.bfloat16
     return pl.pallas_call(
-        functools.partial(sum_kernel, n_wide, count),
-        out_shape=jax.ShapeDtypeStruct((count, rows, width), jnp.float32),
-        in_specs=[pl.BlockSpec(memory_space=pltpu.VMEM)] * count,
-        out_specs=pl.BlockSpec(memory_space=pltpu.VMEM),
+        functools.partial(sum_kernel, n_wide, count, parts, site_count, scale),
+        out_shape=[jax.ShapeDtypeStruct((full_rows, width), jnp.float32)] * count,
+        in_specs=[pl.BlockSpec(memory_space=pltpu.VMEM)] * 8,
+        out_specs=[pl.BlockSpec(memory_space=pltpu.VMEM)] * count,
         scratch_shapes=[
-            pltpu.VMEM((count, levels, 2, rows, 3 * third), bf16),
-            pltpu.VMEM((count, levels, 2, rows, third), bf16),
-            pltpu.VMEM((count, levels, rows, 2 * third), bf16),
-            pltpu.VMEM((count, levels - 1, rows, 2 * third), bf16),
-            pltpu.VMEM((count, rows, 2 * third), bf16),
-            pltpu.VMEM((count, rows, 2 * third), bf16),
-            pltpu.VMEM((count, rows, 3 * third), bf16),
-            pltpu.VMEM((count, rows, 3 * third), bf16),
-            *([dma((count,))] * 6),
-            *([dma((count, levels - 1))] * 2),
-            *([dma((count,))] * 4),
+            *([pltpu.VMEM((tokens, width), bf16)] * 3),
+            *([pltpu.VMEM((chunks, levels, 2, rows, 3 * third), bf16)] * 2),
+            pltpu.VMEM((chunks, levels, 2, rows, third), bf16),
+            pltpu.VMEM((chunks, levels, rows, 2 * third), bf16),
+            pltpu.VMEM((chunks, levels - 1, rows, 2 * third), bf16),
+            pltpu.VMEM((chunks, rows, 2 * third), bf16),
+            pltpu.VMEM((chunks, rows, 2 * third), bf16),
+            pltpu.VMEM((chunks, rows, 3 * third), bf16),
+            pltpu.VMEM((chunks, rows, 3 * third), bf16),
+            *([dma((chunks,))] * 6),
+            *([dma((chunks, levels - 1))] * 2),
+            *([dma((chunks,))] * 4),
         ],
         compiler_params=pltpu.CompilerParams(
             collective_id=1, has_side_effects=True, vmem_limit_bytes=60 * 1024 * 1024
         ),
+        cost_estimate=pl.CostEstimate(
+            flops=2 * count * tokens * width * width, bytes_accessed=200_000_000, transcendentals=0
+        ),
         name="sum_terms",
-    )(*[t.reshape(levels, 2, rows, width) for t in terms])
+    )(q, k, v, d_att, mask, normed_t, attended_t, upstream)
 
 
 def body(
@@ -396,9 +450,10 @@
         (jnp.dot(normed, rows_now, preferred_element_type=jnp.float32) for rows_now in weight_rows)
     )
     head_shape = (clip_count * slab_frames, site_count, head_count, HEAD_DIM)
-    query_heads = query.astype(jnp.bfloat16).reshape(head_shape)
-    key_heads = keys.astype(jnp.bfloat16).reshape(head_shape)
-    value_heads = values.astype(jnp.bfloat16).reshape(head_shape)
+    query, keys, values = (a.astype(jnp.bfloat16) for a in (query, keys, values))
+    query_heads = query.reshape(head_shape)
+    key_heads = keys.reshape(head_shape)
+    value_heads = values.reshape(head_shape)
     scores = (
         jnp.einsum("bshd,buhd->bhsu", query_heads, key_heads, preferred_element_type=jnp.float32)
         * scale
@@ -432,39 +487,23 @@
     upstream = jnp.where(
         live_rows[:, None], clip_grad.reshape(-1, model_width), jnp.zeros((), jnp.bfloat16)
     )
-    term_output = jnp.einsum("rk,rd->kd", attended, upstream, preferred_element_type=jnp.float32)
     d_attended = jnp.einsum(
         "rd,kd->rk", upstream, output_full, preferred_element_type=jnp.float32
     ).astype(jnp.bfloat16)
-    d_att_heads = d_attended.reshape(head_shape)
-    d_probs = jnp.einsum(
-        "bshd,buhd->bhsu", d_att_heads, value_heads, preferred_element_type=jnp.float32
-    )
-    inner = jnp.sum(probs * d_probs, axis=-1, keepdims=True)
-    d_scores = (probs * (d_probs - inner) * scale).astype(jnp.bfloat16)
-    d_query = (
-        jnp.einsum("bhsu,buhd->bshd", d_scores, key_heads, preferred_element_type=jnp.float32)
-        .astype(jnp.bfloat16)
-        .reshape(-1, model_width)
-    )
-    d_keys = (
-        jnp.einsum("bhsu,bshd->buhd", d_scores, query_heads, preferred_element_type=jnp.float32)
-        .astype(jnp.bfloat16)
-        .reshape(-1, model_width)
-    )
-    d_values = (
-        jnp.einsum("bhsu,bshd->buhd", probs_low, d_att_heads, preferred_element_type=jnp.float32)
-        .astype(jnp.bfloat16)
-        .reshape(-1, model_width)
-    )
-    term_query = jnp.einsum("rk,rd->kd", normed, d_query, preferred_element_type=jnp.float32)
-    term_key = jnp.einsum("rk,rd->kd", normed, d_keys, preferred_element_type=jnp.float32)
-    term_value = jnp.einsum("rk,rd->kd", normed, d_values, preferred_element_type=jnp.float32)
     totals = sum_terms(
         n_wide,
-        *(t.astype(jnp.bfloat16) for t in (term_value, term_key, term_query, term_output)),
-    )
-    return (block_out, totals[2], totals[1], totals[0], totals[3])
+        site_count,
+        scale,
+        query,
+        keys,
+        values,
+        d_attended,
+        key_mask.astype(jnp.float32),
+        normed.T,
+        attended.T,
+        upstream,
+    )
+    return (block_out, totals[3], totals[2], totals[1], totals[0])
 
 
 def solution(mesh):

time: 330 us -> 326 us (0.988)
  matrix products: 51.3 us -> 35.5 us
  local copies, waits for them, and re-layouts: 25 us -> 33.2 us
  Pallas kernels: 229 us -> 234 us
    dot_general x8 -> x1, matrix products: 27.8 us -> 3.24 us  [body(): jnp.einsum('bshd,buhd->bhsu', query_heads, key_heads, preferred_element_t...]
    unnamed x51 -> x46, local copies, waits for them, and re-layouts: 8.6 us -> 16.4 us
    dot_general x3, matrix products: 6.88 us -> 12 us  [body(): jnp.dot(normed, rows_now, preferred_element_type=jnp.float32)]
    squeeze x1 -> x0, local copies, waits for them, and re-layouts: 4.59 us -> none  [body(): return (block_out, totals[2], totals[1], totals[0], totals[3])]
    pallas_call x1, Pallas kernels: 138 us -> 142 us  [sum_terms(): pl.pallas_call(functools.partial(sum_kernel, n_wide, count, parts, site_c...]
    reshape x4, local copies, waits for them, and re-layouts: 4.97 us -> 9.42 us  [the longest x1 2.37 us: body(): query_heads = query.reshape(head_shape)]
  transfers between devices with their start and end apart: 3 -> 3, of which waited for: 0 -> 0; matrix products, arithmetic and copies ran while one was open for 21% -> 17% of each run, Pallas kernels for 70% -> 72%
where the time goes in v2:
time: 326 us; the launch traced here: 325 us
  Pallas kernels  234 us (72%)
  matrix products  35.5 us (11%)
  local copies, waits for them, and re-layouts  33.2 us (10%)
  starting transfers between devices  13.8 us (4%)
  between operations  4.82 us (1%)
  other arithmetic  3.29 us (1%)
    pallas_call x1, Pallas kernels, sum_terms(): pl.pallas_call(functools.partial(sum_kernel, n_wide, count, parts, site_c...  142 us
    pallas_call x1, Pallas kernels, gather_weights(): pl.pallas_call(functools.partial(gather_kernel, n_wide, count), out_shape...  91.9 us
    unnamed x46, local copies, waits for them, and re-layouts  16.4 us
    dot_general x3, matrix products, body(): jnp.dot(normed, rows_now, preferred_element_type=jnp.float32)  12 us
  transfers between devices with their start and end apart: 3, of which 0 were waited for; matrix products, arithmetic and copies ran while one was open for 17% of the time, Pallas kernels for 72%

profile of v2, /device:TPU:0, one launch (start us, length us, event | category | flops | bytes accessed | tf_op | source)
XLA Modules:
  0.0 324.5 jit_solution(9791319211921876470)
XLA Ops:
  0.6 0.0 copy-start
  0.6 5.7 %collective-permute-start = (bf16[2,2,64,512]{3,2,1,0:T(8,128)(2,1)}, bf16[2,2,64,512]{3,2,1,0:T(8,128)(2,1)}, u32[]{:S(2)}, u32[]{:S(2)}) collective-permute-start(bf16[2,2,64,512]{3,2,1,0:T(8,128)(2,1)} %bitcast.68), channel_id=1, source_target_pairs={{0,1},{1,2},{2,3},{3,4},{4,5},{5,6},{6,7},{8,9},{9,10},{10,11},{11... | collective-permute-start | bytes 786440 | tf_op jit(solution)/shard_map/ppermute | solution.py:23
  6.4 4.5 %all-to-all-start.1 = ((bf16[4,2,64,1536]{3,2,1,0:T(8,128)(2,1)}), bf16[4,2,64,1536]{3,2,1,0:T(8,128)(2,1)}, u32[]{:S(2)}, u32[]{:S(2)}) async-start(bf16[4,2,64,1536]{3,2,1,0:T(8,128)(2,1)} %bitcast.64), calls=%async_computation.1 | async-start | bytes 3145728 | tf_op jit(solution)/shard_map/all_to_all | solution.py:436
  11.0 0.2 select_reduce_fusion
  11.2 0.1 multiply_reduce_fusion.3
  11.3 0.1 iota_compare_fusion.2
  11.4 0.1 broadcast_compare_fusion
  11.5 0.1 broadcast_and_fusion
  11.6 0.6 fusion.36
  14.7 0.1 broadcast_in_dim.58
  14.8 0.1 lt.69
  14.9 0.1 and.25
  16.3 0.0 copy-done.1
  16.3 0.0 copy-start.4
  16.3 1.1 copy-done.4
  17.4 91.9 %gather_weights.1 = (bf16[1536,1536]{1,0:T(8,128)(2,1)S(1)}, bf16[1536,1536]{1,0:T(8,128)(2,1)S(1)}, bf16[1536,1536]{1,0:T(8,128)(2,1)S(1)}, bf16[1536,1536]{1,0:T(8,128)(2,1)S(1)}) custom-call(bf16[192,1536]{1,0:T(8,128)(2,1)S(1)} %copy-done.1, bf16[192,1536]{1,0:T(8,128)(2,1)S(1)} %copy-done.2, bf16[192,1536]{1,0:T(8,128)(2,1)S(1)} %copy-done.3, ...), custom_call_target="tpu_custom_call" | custom-call | tf_op jit(solution)/shard_map/gather_weights/pallas_call | solution.py:163
  109.3 2.1 copy-done.6
  111.4 2.2 copy-done.7
  113.7 0.8 fusion.32
  114.5 0.0 collective-permute-done
  114.5 0.3 convolution_add_fusion.3
  114.8 1.0 copy-done.5
  115.8 1.2 convolution_add_fusion.2
  117.0 1.3 fusion.7
  118.3 0.7 fusion.37
  119.0 0.3 multiply_reduce_fusion
  119.3 0.2 multiply_convert_fusion
  119.6 0.0 copy-start.13
  119.6 0.9 copy-done.13
  120.4 2.3 convolution_convert_fusion.4.refs_0_
  122.7 2.4 reshape.160
  125.1 4.8 %convolution_convert_fusion.3.refs_1_ = bf16[256,1536]{1,0:T(8,128)(2,1)} fusion(bf16[256,1536]{1,0:T(8,128)(2,1)} %copy-done.13, bf16[1536,1536]{1,0:T(8,128)(2,1)} %copy-done.7), kind=kOutput, calls=%fused_computation.7 | convolution fusion | flops 1208352768 | bytes 6291456 | tf_op jit(solution)/shard_map/dot_general | solution.py:450
  129.9 2.4 reshape.161
  132.3 3.2 multiply_select_fusion
  135.6 2.4 fusion.38
  138.0 4.9 %convolution_convert_fusion.5.refs_2_ = bf16[256,1536]{1,0:T(8,128)(2,1)} fusion(bf16[256,1536]{1,0:T(8,128)(2,1)} %copy-done.13, bf16[1536,1536]{1,0:T(8,128)(2,1)} %copy-done.6), kind=kOutput, calls=%fused_computation.9 | convolution fusion | flops 1208352768 | bytes 6291456 | tf_op jit(solution)/shard_map/dot_general | solution.py:450
  142.8 2.4 reshape.159
  145.2 3.7 %fusion.6 = bf16[4,64,12,128]{3,1,2,0:T(8,128)(2,1)} fusion(bf16[4,64,12,128]{3,2,1,0:T(8,128)(2,1)} %reshape.159, f32[4,12,64]{2,1,0:T(8,128)S(1)} %fusion.38, f32[4,12,64,64]{2,3,1,0:T(8,128)} %multiply_select_fusion), kind=kOutput, calls=%fused_computation.20 | convolution fusion | flops 51317824 | bytes 2371584 | tf_op jit(solution)/shard_map/bhsu,buhd->bshd/dot_general | solution.py:468
  148.9 1.7 copy.50
  150.6 1.1 copy.78
  151.7 2.3 copy.53
  154.0 1.1 fusion.56
  155.1 2.3 copy.54.refs_5_
  157.4 4.0 %fusion.3 = bf16[256,1536]{1,0:T(8,128)(2,1)S(1)} fusion(f32[256,1536]{1,0:T(8,128)S(1)} %get-tuple-element.41, bf16[256,1536]{1,0:T(8,128)(2,1)} %bitcast.63, bf16[1536,1536]{1,0:T(8,128)(2,1)} %copy-done.5, pred[256]{0:T(512)(128)(4,1)S(1)} %and.25), kind=kOutput, calls=%fused_computation.10 | convolution fusion | flops 1209139200 | bytes 7864576 | tf_op jit(solution)/shard_map/dot_general | solution.py:472
  161.4 1.7 convolution_convert_fusion
  163.1 1.4 copy.52
  164.5 0.0 all-to-all-done.1
  164.5 3.6 %all-to-all-start = ((bf16[4,2,64,1536]{3,2,1,0:T(8,128)(2,1)}), bf16[4,2,64,1536]{3,2,1,0:T(8,128)(2,1)S(1)}, u32[]{:S(2)}, u32[]{:S(2)}) async-start(bf16[4,2,64,1536]{3,2,1,0:T(8,128)(2,1)} %copy.52), calls=%async_computation | async-start | bytes 3145728 | tf_op jit(solution)/shard_map/all_to_all | solution.py:475
  168.1 1.2 constant_dynamic-slice_fusion
  169.3 0.1 pad_maximum_fusion
  169.4 0.2 bitcast_select_fusion.refs_7_
  169.5 0.0 copy-start.12
  169.6 4.9 %convolution_convert_fusion.2.refs_3_ = bf16[256,1536]{1,0:T(8,128)(2,1)} fusion(bf16[256,1536]{1,0:T(8,128)(2,1)S(1)} %bitcast_select_fusion.refs_7_, bf16[1536,1536]{1,0:T(8,128)(2,1)} %copy-done.5), kind=kOutput, calls=%fused_computation.6 | convolution fusion | flops 1208352768 | bytes 6291456 | tf_op jit(solution)/shard_map/rd,kd->rk/dot_general | solution.py:490
  174.5 142.1 %sum_terms.1 = (f32[192,1536]{1,0:T(8,128)}, f32[192,1536]{1,0:T(8,128)}, f32[192,1536]{1,0:T(8,128)}, f32[192,1536]{1,0:T(8,128)}) custom-call(bf16[256,1536]{1,0:T(8,128)(2,1)} %convolution_convert_fusion.4.refs_0_, bf16[256,1536]{1,0:T(8,128)(2,1)} %convolution_convert_fusion.3.refs_1_, bf16[256,1536]{1,0:T(8,128)(2,1)} %convolution_convert_fusion.5.refs_2_, ...), custom_call_target="tpu_custom_call" | custom-call | flops 4831838208 | bytes 200000000 | tf_op jit(solution)/shard_map/sum_terms/pallas_call | solution.py:357
  316.6 0.0 all-to-all-done
  316.6 1.1 copy.84
  317.7 0.7 copy-done.11
  318.4 1.0 copy.85
  319.4 0.7 copy-done.10
  320.1 1.0 copy.86
  321.1 0.7 copy-done.9
  321.8 1.0 copy.87
  322.8 0.7 copy-done.8
  323.5 1.0 copy.88
  (32 shorter events, 0.1 us)
Async XLA Ops:
  0.6 117.7 %copy-start = (bf16[512,1536]{1,0:T(8,128)(2,1)S(1)}, bf16[512,1536]{1,0:T(8,128)(2,1)}, u32[]{:S(2)}) copy-start(bf16[512,1536]{1,0:T(8,128)(2,1)} %param.14) | copy-start | bytes 4718596
  0.6 113.8 %collective-permute-start = (bf16[2,2,64,512]{3,2,1,0:T(8,128)(2,1)}, bf16[2,2,64,512]{3,2,1,0:T(8,128)(2,1)}, u32[]{:S(2)}, u32[]{:S(2)}) collective-permute-start(bf16[2,2,64,512]{3,2,1,0:T(8,128)(2,1)} %bitcast.68), channel_id=1, source_target_pairs={{0,1},{1,2},{2,3},{3,4},{4,5},{5,6},{6,7},{8,9},{9,10},{10,11},{11... | collective-permute-start | bytes 786440 | tf_op jit(solution)/shard_map/ppermute | solution.py:23
  6.4 4.6 %copy-start.14 = (s32[4,2,2]{0,2,1:T(2,128)S(1)}, s32[4,2,2]{0,2,1:T(2,128)}, u32[]{:S(2)}) copy-start(s32[4,2,2]{0,2,1:T(2,128)} %param.23) | copy-start | bytes 196
  6.4 4.6 %copy-start.16 = (s32[4,2]{0,1:T(2,128)S(1)}, s32[4,2]{0,1:T(2,128)}, u32[]{:S(2)}) copy-start(s32[4,2]{0,1:T(2,128)} %param.21) | copy-start | bytes 100
  6.4 4.6 %copy-start.17 = (s32[16]{0:T(128)S(1)}, s32[16]{0:T(128)}, u32[]{:S(2)}) copy-start(s32[16]{0:T(128)} %param.20) | copy-start | bytes 196
  6.4 4.8 %copy-start.15 = (s32[4,2]{0,1:T(2,128)S(1)}, s32[4,2]{0,1:T(2,128)}, u32[]{:S(2)}) copy-start(s32[4,2]{0,1:T(2,128)} %param.22) | copy-start | bytes 100
  6.4 9.9 %copy-start.1 = (bf16[192,1536]{1,0:T(8,128)(2,1)S(1)}, bf16[192,1536]{1,0:T(8,128)(2,1)}, u32[]{:S(2)}) copy-start(bf16[192,1536]{1,0:T(8,128)(2,1)} %refs_0_.1) | copy-start | bytes 1769476
  6.4 9.9 %copy-start.2 = (bf16[192,1536]{1,0:T(8,128)(2,1)S(1)}, bf16[192,1536]{1,0:T(8,128)(2,1)}, u32[]{:S(2)}) copy-start(bf16[192,1536]{1,0:T(8,128)(2,1)} %refs_1_.1) | copy-start | bytes 1769476
  6.4 9.9 %copy-start.3 = (bf16[192,1536]{1,0:T(8,128)(2,1)S(1)}, bf16[192,1536]{1,0:T(8,128)(2,1)}, u32[]{:S(2)}) copy-start(bf16[192,1536]{1,0:T(8,128)(2,1)} %refs_2_.1) | copy-start | bytes 1769476
  6.4 158.1 %all-to-all-start.1 = ((bf16[4,2,64,1536]{3,2,1,0:T(8,128)(2,1)}), bf16[4,2,64,1536]{3,2,1,0:T(8,128)(2,1)}, u32[]{:S(2)}, u32[]{:S(2)}) async-start(bf16[4,2,64,1536]{3,2,1,0:T(8,128)(2,1)} %bitcast.64), calls=%async_computation.1 | async-start | bytes 3145728 | tf_op jit(solution)/shard_map/all_to_all | solution.py:436
  16.3 1.1 copy-start.4
  17.4 97.1 %copy-start.18 = (bf16[3,512,512]{2,1,0:T(8,128)(2,1)S(1)}, bf16[3,512,512]{2,1,0:T(8,128)(2,1)}, u32[]{:S(2)}) copy-start(bf16[3,512,512]{2,1,0:T(8,128)(2,1)} %param.13) | copy-start | bytes 4718596
  17.4 97.1 %copy-start.19 = (bf16[1,2,2,64,512]{4,3,2,1,0:T(8,128)(2,1)S(1)}, bf16[1,2,2,64,512]{4,3,2,1,0:T(8,128)(2,1)}, u32[]{:S(2)}) copy-start(bf16[1,2,2,64,512]{4,3,2,1,0:T(8,128)(2,1)} %param.12) | copy-start | bytes 786436
  109.3 2.2 copy-start.6
  111.4 2.2 copy-start.7
  113.7 2.1 copy-start.5
  119.6 0.9 copy-start.13
  164.5 152.0 %all-to-all-start = ((bf16[4,2,64,1536]{3,2,1,0:T(8,128)(2,1)}), bf16[4,2,64,1536]{3,2,1,0:T(8,128)(2,1)S(1)}, u32[]{:S(2)}, u32[]{:S(2)}) async-start(bf16[4,2,64,1536]{3,2,1,0:T(8,128)(2,1)} %copy.52), calls=%async_computation | async-start | bytes 3145728 | tf_op jit(solution)/shard_map/all_to_all | solution.py:475
  169.5 4.9 %copy-start.12 = (bf16[256,1536]{1,0:T(8,128)(2,1)}, bf16[256,1536]{1,0:T(8,128)(2,1)S(1)}, u32[]{:S(2)}) copy-start(bf16[256,1536]{1,0:T(8,128)(2,1)S(1)} %bitcast_select_fusion.refs_7_) | copy-start | bytes 2359300
  316.6 1.8 copy-start.11
  318.4 1.7 copy-start.10
  320.1 1.7 copy-start.9
  321.8 1.7 copy-start.8

commit v3 on v2

--- a/solution.py
+++ b/solution.py
@@ -66,9 +66,11 @@
     )
 
 
-def gather_kernel(n_wide, count, *refs):
-    shards, fulls = refs[:count], refs[count : 2 * count]
-    local_sem, flat_send, flat_recv, across_send, across_recv, core_send, core_recv = refs[2 * count :]
+def gather_kernel(n_wide, count, site_count, scale, *refs):
+    shards, normed_ref, mask_ref = refs[:count], refs[count], refs[count + 1]
+    results, att_ref = refs[count + 2 : 2 * count + 1], refs[2 * count + 1]
+    fulls = (*refs[2 * count + 3 : 3 * count + 2], refs[2 * count + 2])
+    local_sem, flat_send, flat_recv, across_send, across_recv, core_send, core_recv = refs[3 * count + 2 :]
     here = Place(n_wide)
     rows, width = shards[0].shape
     third = width // (CORES * 3)
@@ -123,6 +125,43 @@
                 copy.start()
                 pending.append(copy)
 
+    sibling_cols = pl.ds(pl.multiple_of((1 - here.core) * (3 * third), third), 3 * third)
+    f32, bf16 = jnp.float32, jnp.bfloat16
+
+    def complete(k):
+        for other in range(2):
+            for offset in range(1 - other, levels):
+                arrived(k, block(offset, other), sibling_cols, core_recv.at[k, offset, other])
+        locals_[k].wait()
+
+    def project(k):
+        complete(k)
+
+        @pl.loop(0, width // third)
+        def _(i):
+            lanes = pl.ds(pl.multiple_of(i * third, third), third)
+            results[k][:, lanes] = jnp.dot(
+                normed_ref[...], fulls[k][:, lanes], preferred_element_type=f32
+            ).astype(bf16)
+
+    def attention():
+        q_ref, k_ref, v_ref = results
+
+        @pl.loop(0, width // HEAD_DIM)
+        def _(h):
+            lanes = pl.ds(pl.multiple_of(h * HEAD_DIM, HEAD_DIM), HEAD_DIM)
+            for b in range(normed_ref.shape[0] // site_count):
+                at = pl.ds(b * site_count, site_count)
+                scores = lax.dot_general(
+                    q_ref[at, lanes], k_ref[at, lanes], (((1,), (1,)), ((), ())), preferred_element_type=f32
+                )
+                scores = jnp.where(mask_ref[pl.ds(b, 1), :] > 0, scores * scale, masked_score)
+                weights = jnp.exp(scores - jnp.max(scores, axis=-1, keepdims=True))
+                probs = weights / jnp.sum(weights, axis=-1, keepdims=True)
+                att_ref[at, lanes] = jnp.dot(
+                    probs.astype(bf16), v_ref[at, lanes], preferred_element_type=f32
+                ).astype(bf16)
+
     for k in range(count):
         for other in range(2):
             for offset in range(1 - other, levels):
@@ -143,42 +182,40 @@
                 pending.append(copy)
         if k:
             finish_core(k - 1)
+        if k > 1:
+            project(k - 2)
     finish_core(count - 1)
-    sibling_cols = pl.ds(pl.multiple_of((1 - here.core) * (3 * third), third), 3 * third)
-    for k in range(count):
-        for other in range(2):
-            for offset in range(1 - other, levels):
-                arrived(k, block(offset, other), sibling_cols, core_recv.at[k, offset, other])
-    for copy in locals_:
-        copy.wait()
+    project(count - 2)
+    attention()
+    complete(count - 1)
     for copy in pending:
         copy.wait_send()
 
 
-def gather_weights(n_wide, *shards):
+def gather_weights(n_wide, site_count, scale, normed, mask, *shards):
     count = len(shards)
     rows, width = shards[0].shape
     levels = n_wide // 2
     dma = pltpu.SemaphoreType.DMA
+    vmem = pl.BlockSpec(memory_space=pltpu.VMEM)
+    full = (n_wide * rows, width)
     return pl.pallas_call(
-        functools.partial(gather_kernel, n_wide, count),
-        out_shape=[jax.ShapeDtypeStruct((n_wide * rows, width), s.dtype) for s in shards],
-        in_specs=[pl.BlockSpec(memory_space=pltpu.VMEM)] * count,
-        out_specs=[pl.BlockSpec(memory_space=pl.ANY)] * count,
+        functools.partial(gather_kernel, n_wide, count, site_count, scale),
+        out_shape=[jax.ShapeDtypeStruct(normed.shape, normed.dtype)] * count
+        + [jax.ShapeDtypeStruct(full, shards[0].dtype)],
+        in_specs=[vmem] * (count + 2),
+        out_specs=[vmem] * count + [pl.BlockSpec(memory_space=pl.ANY)],
         scratch_shapes=[
+            *([pltpu.VMEM(full, shards[0].dtype)] * (count - 1)),
             dma((count,)),
             dma((count, 2, levels)),
-            dma((count, levels, 2)),
-            dma((count, levels, 2)),
-            dma((count, levels, 2)),
-            dma((count, levels, 2)),
-            dma((count, levels, 2)),
+            *([dma((count, levels, 2))] * 5),
         ],
         compiler_params=pltpu.CompilerParams(
-            collective_id=0, has_side_effects=True, vmem_limit_bytes=16 * 1024 * 1024
+            collective_id=0, has_side_effects=True, vmem_limit_bytes=40 * 1024 * 1024
         ),
         name="gather_weights",
-    )(*shards)
+    )(*shards, normed, mask)
 
 
 def sum_kernel(n_wide, count, parts, site_count, scale, *refs):
@@ -404,7 +441,6 @@
     frame_slab = frames[0]
     clip_count, slab_frames, site_count, channels = frame_slab.shape
     model_width = embed_weight.shape[1]
-    head_count = model_width // HEAD_DIM
     earlier = from_behind(frame_slab, "wide", 1)
     joined = jnp.concatenate([earlier, frame_slab], axis=1)
     active = jax.nn.silu(joined.astype(jnp.float32)).astype(jnp.bfloat16)
@@ -442,33 +478,11 @@
     ).astype(jnp.bfloat16)
     normed = layer_norm(tokens)
     n_wide = lax.axis_size("wide")
-    query_full, key_full, value_full, output_full = gather_weights(
-        n_wide, query_weight, key_weight, value_weight, output_weight
-    )
-    weight_rows = (query_full, key_full, value_full)
-    query, keys, values = tuple(
-        (jnp.dot(normed, rows_now, preferred_element_type=jnp.float32) for rows_now in weight_rows)
-    )
-    head_shape = (clip_count * slab_frames, site_count, head_count, HEAD_DIM)
-    query, keys, values = (a.astype(jnp.bfloat16) for a in (query, keys, values))
-    query_heads = query.reshape(head_shape)
-    key_heads = keys.reshape(head_shape)
-    value_heads = values.reshape(head_shape)
-    scores = (
-        jnp.einsum("bshd,buhd->bhsu", query_heads, key_heads, preferred_element_type=jnp.float32)
-        * scale
-    )
     key_limit = jnp.repeat(key_tokens, slab_frames)
-    key_mask = site_pos[None, :] < key_limit[:, None]
-    scores = jnp.where(key_mask[:, None, None, :], scores, masked_score)
-    top = jnp.max(scores, axis=-1, keepdims=True)
-    weights = jnp.exp(scores - top)
-    probs = weights / jnp.sum(weights, axis=-1, keepdims=True)
-    probs_low = probs.astype(jnp.bfloat16)
-    attended = jnp.einsum(
-        "bhsu,buhd->bshd", probs_low, value_heads, preferred_element_type=jnp.float32
-    ).astype(jnp.bfloat16)
-    attended = attended.reshape(-1, model_width)
+    key_mask = (site_pos[None, :] < key_limit[:, None]).astype(jnp.float32)
+    query, keys, values, attended, output_full = gather_weights(
+        n_wide, site_count, scale, normed, key_mask, query_weight, key_weight, value_weight, output_weight
+    )
     projected = jnp.dot(attended, output_full, preferred_element_type=jnp.float32)
     block = (tokens.astype(jnp.float32) + projected).astype(jnp.bfloat16)
     block = jnp.where(live_rows[:, None], block, jnp.zeros((), jnp.bfloat16))
@@ -498,7 +512,7 @@
         keys,
         values,
         d_attended,
-        key_mask.astype(jnp.float32),
+        key_mask,
         normed.T,
         attended.T,
         upstream,

time: 326 us -> 309 us (0.948)
  matrix products: 35.5 us -> 15.4 us
  Pallas kernels: 234 us -> 251 us
  local copies, waits for them, and re-layouts: 33.2 us -> 21 us
    dot_general x5 -> x0, matrix products: 18.9 us -> none  [the longest x3 12 us: body(): jnp.dot(normed, rows_now, preferred_element_type=jnp.float32)]
    pallas_call x1, Pallas kernels: 91.9 us -> 110 us  [gather_weights(): pl.pallas_call(functools.partial(gather_kernel, n_wide, count, site_count...]
    reshape x4 -> x0, local copies, waits for them, and re-layouts: 9.42 us -> none  [the longest x1 2.37 us: body(): query_heads = query.reshape(head_shape)]
    unnamed x46 -> x49, local copies, waits for them, and re-layouts: 16.4 us -> 14.1 us
  transfers between devices with their start and end apart: 3 -> 3, of which waited for: 0 -> 0; matrix products, arithmetic and copies ran while one was open for 17% -> 8% of each run, Pallas kernels for 72% -> 81%
where the time goes in v3:
time: 309 us
  Pallas kernels  251 us (81%)
  local copies, waits for them, and re-layouts  21 us (7%)
  matrix products  15.4 us (5%)
  starting transfers between devices  13.8 us (4%)
  between operations  4.81 us (2%)
    pallas_call x1, Pallas kernels, sum_terms(): pl.pallas_call(functools.partial(sum_kernel, n_wide, count, parts, site_c...  141 us
    pallas_call x1, Pallas kernels, gather_weights(): pl.pallas_call(functools.partial(gather_kernel, n_wide, count, site_count...  110 us
    unnamed x49, local copies, waits for them, and re-layouts  14.1 us
  transfers between devices with their start and end apart: 3, of which 0 were waited for; matrix products, arithmetic and copies ran while one was open for 8% of the time, Pallas kernels for 81%

profile of v3, /device:TPU:0, one launch (start us, length us, event | category | flops | bytes accessed | tf_op | source)
XLA Modules:
  0.0 308.7 jit_solution(8609822341770397972)
XLA Ops:
  0.6 0.0 copy-start
  0.6 0.0 copy-start.21
  0.7 0.0 copy-start.16
  0.7 0.0 copy-start.18
  0.7 0.0 copy-start.19
  0.7 0.0 copy-start.17
  0.7 4.5 %all-to-all-start.1 = ((bf16[4,2,64,1536]{3,2,1,0:T(8,128)(2,1)}), bf16[4,2,64,1536]{3,2,1,0:T(8,128)(2,1)}, u32[]{:S(2)}, u32[]{:S(2)}) async-start(bf16[4,2,64,1536]{3,2,1,0:T(8,128)(2,1)} %bitcast.47), calls=%async_computation.1 | async-start | bytes 3145728 | tf_op jit(solution)/shard_map/all_to_all | solution.py:472
  5.2 0.0 copy-done.21
  5.2 5.6 %collective-permute-start = (bf16[2,2,64,512]{3,2,1,0:T(8,128)(2,1)S(1)}, bf16[2,2,64,512]{3,2,1,0:T(8,128)(2,1)}, u32[]{:S(2)}, u32[]{:S(2)}) collective-permute-start(bf16[2,2,64,512]{3,2,1,0:T(8,128)(2,1)S(1)} %bitcast.51), channel_id=1, source_target_pairs={{0,1},{1,2},{2,3},{3,4},{4,5},{5,6},{6,7},{8,9},{9,10},{10,11},{11... | collective-permute-start | bytes 786440 | tf_op jit(solution)/shard_map/ppermute | solution.py:23
  10.8 0.0 copy-done.16
  10.8 0.0 copy-done.18
  10.8 0.0 copy-done.19
  10.8 0.2 select_reduce_fusion
  11.0 0.0 copy-done.17
  11.0 0.1 multiply_reduce_fusion.3
  11.2 0.1 iota_compare_fusion.2
  11.3 0.1 broadcast_compare_fusion
  11.3 0.1 broadcast_and_fusion
  11.4 0.6 fusion.23
  14.6 0.1 and.25
  14.7 0.1 broadcast_in_dim.26
  14.8 0.1 lt.65
  16.1 0.1 fusion.15.refs_5_.refs_4_
  16.2 0.0 collective-permute-done
  16.2 1.5 convolution_add_fusion.3
  17.7 0.1 copy-done.20
  17.8 1.2 convolution_add_fusion.2
  19.0 1.3 fusion.3
  20.3 0.7 fusion.24
  21.0 0.3 multiply_reduce_fusion
  21.3 1.1 fusion.31
  22.4 2.3 copy.30.refs_5_
  24.8 0.0 copy-start.4
  24.8 0.2 multiply_convert_fusion.refs_4_
  25.0 0.8 copy-done.1
  25.8 0.2 copy-done.2
  26.0 0.2 copy-done.3
  26.2 0.2 copy-done.4
  26.4 109.8 %gather_weights.1 = (bf16[256,1536]{1,0:T(8,128)(2,1)S(1)}, bf16[256,1536]{1,0:T(8,128)(2,1)S(1)}, bf16[256,1536]{1,0:T(8,128)(2,1)S(1)}, bf16[256,1536]{1,0:T(8,128)(2,1)S(1)}, bf16[1536,1536]{1,0:T(8,128)(2,1)S(1)}) custom-call(bf16[192,1536]{1,0:T(8,128)(2,1)S(1)} %copy-done.1, bf16[192,1536]{1,0:T(8,128)(2,1)S(1)} %copy-done.2, ...), custom_call_target="tpu_custom_call" | custom-call | tf_op jit(solution)/shard_map/gather_weights/pallas_call | solution.py:202
  136.1 2.1 copy-done.6
  138.3 0.9 copy-done.7
  139.1 0.9 copy-done.8
  140.0 0.9 copy-done.9
  140.9 1.1 copy.29
  142.0 4.2 %fusion.2 = bf16[256,1536]{1,0:T(8,128)(2,1)S(1)} fusion(f32[256,1536]{1,0:T(8,128)} %copy-done.10, bf16[256,1536]{1,0:T(8,128)(2,1)S(1)} %get-tuple-element.14, bf16[1536,1536]{1,0:T(8,128)(2,1)} %copy-done.6, pred[256]{0:T(512)(128)(4,1)S(1)} %and.25), kind=kOutput, calls=%fused_computation.6 | convolution fusion | flops 1209139200 | bytes 7864576 | tf_op jit(solution)/shard_map/dot_general | solution.py:486
  146.3 1.5 convolution_convert_fusion
  147.8 1.4 copy.28
  149.3 0.0 all-to-all-done.1
  149.3 3.7 %all-to-all-start = ((bf16[4,2,64,1536]{3,2,1,0:T(8,128)(2,1)}), bf16[4,2,64,1536]{3,2,1,0:T(8,128)(2,1)S(1)}, u32[]{:S(2)}, u32[]{:S(2)}) async-start(bf16[4,2,64,1536]{3,2,1,0:T(8,128)(2,1)} %copy.28), calls=%async_computation | async-start | bytes 3145728 | tf_op jit(solution)/shard_map/all_to_all | solution.py:489
  153.0 1.2 constant_dynamic-slice_fusion
  154.2 0.1 pad_maximum_fusion
  154.3 0.2 bitcast_select_fusion.refs_7_
  154.4 4.9 %convolution_convert_fusion.2.refs_3_ = bf16[256,1536]{1,0:T(8,128)(2,1)} fusion(bf16[256,1536]{1,0:T(8,128)(2,1)S(1)} %bitcast_select_fusion.refs_7_, bf16[1536,1536]{1,0:T(8,128)(2,1)} %copy-done.6), kind=kOutput, calls=%fused_computation.5 | convolution fusion | flops 1208352768 | bytes 6291456 | tf_op jit(solution)/shard_map/rd,kd->rk/dot_general | solution.py:504
  159.4 141.4 %sum_terms.1 = (f32[192,1536]{1,0:T(8,128)}, f32[192,1536]{1,0:T(8,128)}, f32[192,1536]{1,0:T(8,128)}, f32[192,1536]{1,0:T(8,128)}) custom-call(bf16[256,1536]{1,0:T(8,128)(2,1)} %copy-done.7, bf16[256,1536]{1,0:T(8,128)(2,1)} %copy-done.8, bf16[256,1536]{1,0:T(8,128)(2,1)} %copy-done.9, bf16[256,1536]{1,0:T(8,128)(2,1)} %convolution_convert_fusion.2.refs_3_, ...), custom_call_target="tpu_custom_call" | custom-call | flops 4831838208 | bytes 200000000 | tf_op jit(solution)/shard_map/sum_terms/pallas_call | solution.py:394
  300.8 0.0 all-to-all-done
  300.8 1.1 copy.42
  301.9 0.7 copy-done.14
  302.6 1.0 copy.43
  303.6 0.7 copy-done.13
  304.3 1.0 copy.44
  305.3 0.7 copy-done.12
  306.0 1.0 copy.45
  307.0 0.7 copy-done.11
  307.7 1.0 copy.46
  (25 shorter events, 0.1 us)
Async XLA Ops:
  0.6 19.7 %copy-start = (bf16[512,1536]{1,0:T(8,128)(2,1)S(1)}, bf16[512,1536]{1,0:T(8,128)(2,1)}, u32[]{:S(2)}) copy-start(bf16[512,1536]{1,0:T(8,128)(2,1)} %param.14) | copy-start | bytes 4718596
  0.6 4.5 %copy-start.21 = (bf16[1,2,2,64,512]{4,3,2,1,0:T(8,128)(2,1)S(1)}, bf16[1,2,2,64,512]{4,3,2,1,0:T(8,128)(2,1)}, u32[]{:S(2)}) copy-start(bf16[1,2,2,64,512]{4,3,2,1,0:T(8,128)(2,1)} %param.12) | copy-start | bytes 786436
  0.7 10.1 %copy-start.16 = (s32[4,2,2]{0,2,1:T(2,128)S(1)}, s32[4,2,2]{0,2,1:T(2,128)}, u32[]{:S(2)}) copy-start(s32[4,2,2]{0,2,1:T(2,128)} %param.23) | copy-start | bytes 196
  0.7 10.1 %copy-start.18 = (s32[4,2]{0,1:T(2,128)S(1)}, s32[4,2]{0,1:T(2,128)}, u32[]{:S(2)}) copy-start(s32[4,2]{0,1:T(2,128)} %param.21) | copy-start | bytes 100
  0.7 10.1 %copy-start.19 = (s32[16]{0:T(128)S(1)}, s32[16]{0:T(128)}, u32[]{:S(2)}) copy-start(s32[16]{0:T(128)} %param.20) | copy-start | bytes 196
  0.7 10.3 %copy-start.17 = (s32[4,2]{0,1:T(2,128)S(1)}, s32[4,2]{0,1:T(2,128)}, u32[]{:S(2)}) copy-start(s32[4,2]{0,1:T(2,128)} %param.22) | copy-start | bytes 100
  0.7 148.6 %all-to-all-start.1 = ((bf16[4,2,64,1536]{3,2,1,0:T(8,128)(2,1)}), bf16[4,2,64,1536]{3,2,1,0:T(8,128)(2,1)}, u32[]{:S(2)}, u32[]{:S(2)}) async-start(bf16[4,2,64,1536]{3,2,1,0:T(8,128)(2,1)} %bitcast.47), calls=%async_computation.1 | async-start | bytes 3145728 | tf_op jit(solution)/shard_map/all_to_all | solution.py:472
  5.2 11.0 %collective-permute-start = (bf16[2,2,64,512]{3,2,1,0:T(8,128)(2,1)S(1)}, bf16[2,2,64,512]{3,2,1,0:T(8,128)(2,1)}, u32[]{:S(2)}, u32[]{:S(2)}) collective-permute-start(bf16[2,2,64,512]{3,2,1,0:T(8,128)(2,1)S(1)} %bitcast.51), channel_id=1, source_target_pairs={{0,1},{1,2},{2,3},{3,4},{4,5},{5,6},{6,7},{8,9},{9,10},{10,11},{11... | collective-permute-start | bytes 786440 | tf_op jit(solution)/shard_map/ppermute | solution.py:23
  16.2 8.8 %copy-start.5 = (f32[4,64]{1,0:T(4,128)}, f32[4,64]{1,0:T(4,128)S(1)}, u32[]{:S(2)}) copy-start(f32[4,64]{1,0:T(4,128)S(1)} %fusion.15.refs_5_.refs_4_) | copy-start | bytes 3076
  16.2 1.6 copy-start.20
  21.0 3.8 %copy-start.10 = (f32[256,1536]{1,0:T(8,128)}, f32[256,1536]{1,0:T(8,128)S(1)}, u32[]{:S(2)}) copy-start(f32[256,1536]{1,0:T(8,128)S(1)} %get-tuple-element.36) | copy-start | bytes 4718596
  24.8 1.1 copy-start.1
  24.8 1.2 copy-start.2
  24.8 1.4 copy-start.3
  24.8 1.6 copy-start.4
  136.1 2.1 copy-start.6
  138.3 0.9 copy-start.7
  139.1 0.9 copy-start.8
  140.0 0.9 copy-start.9
  149.3 151.5 %all-to-all-start = ((bf16[4,2,64,1536]{3,2,1,0:T(8,128)(2,1)}), bf16[4,2,64,1536]{3,2,1,0:T(8,128)(2,1)S(1)}, u32[]{:S(2)}, u32[]{:S(2)}) async-start(bf16[4,2,64,1536]{3,2,1,0:T(8,128)(2,1)} %copy.28), calls=%async_computation | async-start | bytes 3145728 | tf_op jit(solution)/shard_map/all_to_all | solution.py:489
  154.4 4.9 %copy-start.15 = (bf16[256,1536]{1,0:T(8,128)(2,1)}, bf16[256,1536]{1,0:T(8,128)(2,1)S(1)}, u32[]{:S(2)}) copy-start(bf16[256,1536]{1,0:T(8,128)(2,1)S(1)} %bitcast_select_fusion.refs_7_) | copy-start | bytes 2359300
  300.8 1.8 copy-start.14
  302.6 1.7 copy-start.13
  304.3 1.7 copy-start.12
  306.0 1.7 copy-start.11
